TPU v7x, 512 devices: a whole 4x8x8 slice. The times are simulated.
512 devices in a mesh: cfg: 2 (over core), seq: 64 (over x, z, y_hi), tp: 4 (over y_lo).
Axes of the slice: x: 4, y: 8 (y_hi: 2, y_lo: 4; y = y_hi * 4 + y_lo), z: 8, core: 2. Of those that a mesh axis runs over, the one named last changes fastest.
Arguments:
- stream: bfloat16 [2, 2560, 3072], P('cfg', 'seq', 'tp'), may hold values from -6 to 6
- queries: bfloat16 [2, 2560, 1536], P('cfg', 'seq', 'tp'), may hold values from -6 to 6
- keys: bfloat16 [2, 2560, 1536], P('cfg', 'seq', 'tp'), may hold values from -6 to 6
- values: bfloat16 [2, 2560, 1536], P('cfg', 'seq', 'tp'), may hold values from -6 to 6
- text_keys: bfloat16 [2, 226, 1536], P('cfg', None, 'tp'), may hold values from -6 to 6
- text_values: bfloat16 [2, 226, 1536], P('cfg', None, 'tp'), may hold values from -6 to 6
- out_weight: bfloat16 [1536, 3072], P('tp'), may hold values from -0.15625 to 0.15625
- gate: float32 [3072], P('tp'), may hold values from -4 to 4
- shift: float32 [3072], P('tp'), may hold values from -3 to 3
- scale: float32 [3072], P('tp'), may hold values from -3 to 3
- proj_weight: float32 [3072, 64], P('tp'), may hold values from -0.109375 to 0.109375
- q_gain: float32 [64], replicated, may hold values from 1.4 to 6
- k_gain: float32 [64], replicated, may hold values from 1.4 to 6
- lengths: int32 [64], replicated, may hold values from 1 to 40, 2304 in all
- latents: float32 [2560, 64], P('seq', ('cfg', 'tp')), may hold values from -6 to 6
- alphas: float32 [1000], replicated, may hold values from 0.05 to 0.95
- step_index: int32 [1], replicated, may hold values from 20 to 999
Outputs:
- hidden_out: bfloat16 [2, 2560, 3072], P('cfg', 'seq', 'tp')
- latents_out: float32 [2560, 64], P('seq', ('cfg', 'tp'))
Inputs may be any that keep to these rules, and one draw needn't show every extreme that they name: `lengths`: video tokens held by each index of seq, in token order; they sum to 2304 and the largest is exactly 40. The previous step's entry is step_index - 20.
All inputs are finite; a program needn't handle non-finite values.
Results may differ from a plain program's by a relative error of at most 0.012.
The roundings to bfloat16 on the way count: a program that leaves them out, or rounds other values in their place, can miss the bound.
Values may be sent and summed in bfloat16 or wider, within the bound.
A program may use at most 64 MiB of HBM per device.

v0:
```python
import jax
import jax.numpy as jnp
from jax import lax
from jax.sharding import PartitionSpec as P

D = 3072
HEAD = 64
HP = 30
WP = 45
STRIDE = 20


guide_scale = 6.0
head_eps = 1e-06
final_eps = 1e-05


def partner_2(shard, axis, distance):
    return lax.ppermute(shard, axis, [(i, i ^ 1 << distance) for i in range(lax.axis_size(axis))])


def rope_tables(position):
    frame = position // (HP * WP)
    height = position // WP % HP
    across = position % WP

    def angles(coord, extent):
        freq = 1.0 / 10000.0 ** (jnp.arange(0, extent, 2, dtype=jnp.float32) / extent)
        return coord.astype(jnp.float32)[:, None] * freq[None, :]

    angle = jnp.concatenate([angles(frame, 16), angles(height, 24), angles(across, 24)], axis=1)
    return (jnp.cos(angle), jnp.sin(angle))


def head_norm(field, gain):
    centre = field - jnp.mean(field, axis=-1, keepdims=True)
    spread = jnp.mean(centre * centre, axis=-1, keepdims=True)
    return centre * lax.rsqrt(spread + head_eps) * gain


def rotate_pairs(field, cos_table, sin_table):
    pairs = field.reshape(field.shape[:-1] + (HEAD // 2, 2))
    first = pairs[..., 0]
    second = pairs[..., 1]
    cos_part = cos_table[:, None, :]
    sin_part = sin_table[:, None, :]
    turned = jnp.stack(
        [first * cos_part - second * sin_part, second * cos_part + first * sin_part], axis=-1
    )
    return turned.reshape(field.shape)


def prepare(field, gain, tables):
    count = field.shape[0]
    normed = head_norm(field.astype(jnp.float32).reshape(count, -1, HEAD), gain)
    if tables is not None:
        normed = rotate_pairs(normed, tables[0], tables[1])
    return normed.reshape(count, -1).astype(jnp.bfloat16)


def last_dims(left, right):
    return lax.dot_general(
        left, right, (((1,), (1,)), ((), ())), preferred_element_type=jnp.float32
    )


def shards(
    stream,
    queries,
    keys,
    values,
    text_keys,
    text_values,
    out_weight,
    gate,
    shift,
    scale,
    proj_weight,
    q_gain,
    k_gain,
    lengths,
    latents,
    alphas,
    step_index,
):
    blocks = lax.axis_size("seq")
    group = lax.axis_size("tp")
    rows = queries.shape[1]
    width = queries.shape[2]
    heads_here = width // HEAD
    seq_rank = lax.axis_index("seq")
    order = jnp.arange(blocks, dtype=jnp.int32)
    own_start = jnp.sum(jnp.where(order < seq_rank, lengths, 0))
    own_count = jnp.sum(jnp.where(order == seq_rank, lengths, 0))
    within = jnp.arange(rows, dtype=jnp.int32)
    own_live = within < own_count
    own_tables = rope_tables(own_start + within)
    query_hat = prepare(queries[0], q_gain, own_tables)
    outgoing = keys[0]
    arrived_keys, arrived_values = (
        lax.all_gather(outgoing, "seq", axis=0, tiled=True),
        lax.all_gather(values[0], "seq", axis=0, tiled=True),
    )
    offsets = jnp.cumsum(lengths) - lengths
    all_positions = (offsets[:, None] + within[None, :]).reshape(-1)
    video_keys = prepare(arrived_keys, k_gain, rope_tables(all_positions))
    video_live = (within[None, :] < lengths[:, None]).reshape(-1)
    text_hat = prepare(text_keys[0], k_gain, None)
    text_vals = text_values[0]

    def one_head(head):
        start = head * HEAD
        query_part = lax.dynamic_slice_in_dim(query_hat, start, HEAD, 1)
        video_key_part = lax.dynamic_slice_in_dim(video_keys, start, HEAD, 1)
        video_value_part = lax.dynamic_slice_in_dim(arrived_values, start, HEAD, 1)
        text_key_part = lax.dynamic_slice_in_dim(text_hat, start, HEAD, 1)
        text_value_part = lax.dynamic_slice_in_dim(text_vals, start, HEAD, 1)
        video_scores = last_dims(query_part, video_key_part) * 0.125
        video_scores = jnp.where(video_live[None, :], video_scores, -jnp.inf)
        text_scores = last_dims(query_part, text_key_part) * 0.125
        row_max = jnp.maximum(
            jnp.max(video_scores, axis=1, keepdims=True),
            jnp.max(text_scores, axis=1, keepdims=True),
        )
        video_weights = jnp.exp(video_scores - row_max)
        text_weights = jnp.exp(text_scores - row_max)
        totals = jnp.sum(video_weights, axis=1, keepdims=True) + jnp.sum(
            text_weights, axis=1, keepdims=True
        )
        mixed = jnp.dot(
            video_weights.astype(jnp.bfloat16), video_value_part, preferred_element_type=jnp.float32
        )
        mixed = mixed + jnp.dot(
            text_weights.astype(jnp.bfloat16), text_value_part, preferred_element_type=jnp.float32
        )
        return (mixed / totals).astype(jnp.bfloat16)

    attended = lax.map(one_head, jnp.arange(heads_here, dtype=jnp.int32))
    attended = jnp.transpose(attended, (1, 0, 2)).reshape(rows, width)
    projected = jnp.dot(attended, out_weight, preferred_element_type=jnp.float32)
    summed = lax.psum_scatter(
        projected.astype(jnp.bfloat16), "tp", scatter_dimension=1, tiled=True
    ).astype(jnp.float32)
    hidden = stream[0].astype(jnp.float32) + gate * summed
    hidden = jnp.where(own_live[:, None], hidden, 0.0).astype(jnp.bfloat16)
    widened = lax.optimization_barrier(hidden).astype(jnp.float32)
    row_total, row_square = lax.psum(
        (jnp.sum(widened, axis=1), jnp.sum(widened * widened, axis=1)), "tp"
    )
    mean = row_total[:, None] / D
    square = row_square[:, None] / D
    normed = (widened - mean) * lax.rsqrt(square - mean * mean + final_eps) * (1.0 + scale) + shift
    partial_pred = jnp.dot(
        normed, proj_weight, precision=lax.Precision.HIGHEST, preferred_element_type=jnp.float32
    )
    cfg_rank = lax.axis_index("cfg")
    tp_rank = lax.axis_index("tp")
    piece = proj_weight.shape[1] // (2 * group)
    prediction = lax.psum(partial_pred, "tp")
    partner = partner_2(prediction, "cfg", 0)
    column = (cfg_rank * group + tp_rank) * piece
    mine = lax.dynamic_slice_in_dim(prediction, column, piece, 1)
    theirs = lax.dynamic_slice_in_dim(partner, column, piece, 1)
    is_conditioned = cfg_rank == 0
    conditioned = jnp.where(is_conditioned, mine, theirs)
    unconditioned = jnp.where(is_conditioned, theirs, mine)
    guided = unconditioned + guide_scale * (conditioned - unconditioned)
    current = alphas[step_index[0]]
    earlier = alphas[step_index[0] - STRIDE]
    root_now = jnp.sqrt(current)
    rest_now = jnp.sqrt(1.0 - current)
    clean = root_now * latents - rest_now * guided
    noise = root_now * guided + rest_now * latents
    stepped = jnp.sqrt(earlier) * clean + jnp.sqrt(1.0 - earlier) * noise
    latents_out = jnp.where(own_live[:, None], stepped, 0.0)
    return (hidden[None], latents_out)


def solution(mesh):
    return jax.shard_map(
        shards,
        mesh=mesh,
        in_specs=(
            P("cfg", "seq", "tp"),
            P("cfg", "seq", "tp"),
            P("cfg", "seq", "tp"),
            P("cfg", "seq", "tp"),
            P("cfg", None, "tp"),
            P("cfg", None, "tp"),
            P("tp", None),
            P("tp"),
            P("tp"),
            P("tp"),
            P("tp", None),
            P(),
            P(),
            P(),
            P("seq", ("cfg", "tp")),
            P(),
            P(),
        ),
        out_specs=(P("cfg", "seq", "tp"), P("seq", ("cfg", "tp"))),
        check_vma=False,
    )
```

profile of v0, /device:TPU:1, one launch (start us, length us, event | category | flops | bytes accessed | tf_op | source)
XLA Modules:
  0.0 389.1 jit_solution(11699721490610072539)
XLA Ops:
  7.2 0.7 all-gather.5.cloned.1.call-update
  8.0 0.7 all-gather.7.cloned.1.call-update
  8.7 0.7 copy.55
  9.7 1.3 fusion.51
  11.2 0.7 fusion.53
  11.9 0.7 fusion.57
  12.6 0.9 reshape.432
  13.4 0.9 copy.50
  14.8 0.8 mul.360
  16.3 0.8 mul.340
  18.6 1.4 fusion.29
  20.0 127.2 %all-gather.5.cloned.1.call-done = bf16[1,2560,384]{2,1,0:T(8,128)(2,1)} async-done(((bf16[1,40,384]{2,1,0:T(8,128)(2,1)}), bf16[1,2560,384]{2,1,0:T(8,128)(2,1)}) %all-gather.5.cloned.1.call-update) | async-done | bytes 1966096 | tf_op jit(solution)/shard_map/all_gather | solution.py:101
  147.2 4.0 %copy.54 = bf16[1,2560,384]{1,2,0:T(8,128)(2,1)} copy(bf16[1,2560,384]{2,1,0:T(8,128)(2,1)} %all-gather.5.cloned.1.call-done) | data formatting | bytes 3932160 | tf_op jit(solution)/shard_map/all_gather | solution.py:101
  151.2 3.9 %convert_element_type.154 = f32[1,2560,384]{1,2,0:T(8,128)} convert(bf16[1,2560,384]{1,2,0:T(8,128)(2,1)} %copy.54) | non-fusion elementwise | flops 983040 | bytes 5898240 | tf_op jit(solution)/shard_map/convert_element_type | solution.py:55
  155.1 2.5 reduce_sum.112
  157.6 5.3 %reshape.425 = f32[2560,6,32,2]{0,3,2,1:T(2,128)} reshape(bf16[1,2560,384]{1,2,0:T(8,128)(2,1)} %copy.54) | data formatting | bytes 5898240 | tf_op jit(solution)/shard_map/reshape | solution.py:55
  162.9 2.8 multiply_reduce_fusion
  165.8 0.4 copy-done.1
  166.2 1.8 multiply_multiply_fusion
  168.0 5.2 %subtract_convert_fusion = (bf16[2560,6,32,1]{0,3,2,1:T(2,128)(2,1)S(1)}, bf16[2560,6,32,1]{0,3,2,1:T(2,128)(2,1)S(1)}) fusion(f32[2560,6,32,2]{0,3,2,1:T(2,128)S(1)} %multiply_multiply_fusion, f32[2560,32]{0,1:T(8,128)S(1)} %get-tuple-element.135, f32[2560,32]{0,1:T(8,128)S(1)} %get-tuple-element.134), kind=kLoop, calls=%fused_computation.34 | loop fusion | flops 3932160 | bytes 6553600 | tf_op jit(solution)/shard_map/convert.5
  173.2 5.7 %pad_maximum_fusion = bf16[2560,6,32,2]{0,3,2,1:T(2,128)(2,1)} fusion(bf16[2560,6,32,1]{0,3,2,1:T(2,128)(2,1)S(1)} %get-tuple-element.133, bf16[2560,6,32,1]{0,3,2,1:T(2,128)(2,1)S(1)} %get-tuple-element.132), kind=kLoop, calls=%fused_computation.32 | loop fusion | flops 3932160 | bytes 3932160 | tf_op jit(solution)/shard_map/stack | solution.py:47
  178.9 5.2 %convert_element_type.139 = bf16[2560,384]{0,1:T(8,128)(2,1)} reshape(bf16[2560,6,32,2]{0,3,2,1:T(2,128)(2,1)} %pad_maximum_fusion) | data formatting | bytes 3932160 | tf_op jit(solution)/shard_map/convert_element_type | solution.py:58
  184.1 96.8 %all-gather.7.cloned.1.call-done = bf16[1,2560,384]{2,1,0:T(8,128)(2,1)} async-done(((bf16[1,40,384]{2,1,0:T(8,128)(2,1)}), bf16[1,2560,384]{2,1,0:T(8,128)(2,1)}) %all-gather.7.cloned.1.call-update) | async-done | bytes 1966096 | tf_op jit(solution)/shard_map/all_gather | solution.py:102
  281.0 36.7 %while.11 = (s32[]{:T(128)}, bf16[6,40,64]{2,1,0:T(8,128)(2,1)S(1)}, s32[6]{0:T(128)S(1)}, bf16[40,384]{1,0:T(8,128)(2,1)S(1)}, bf16[2560,384]{0,1:T(8,128)(2,1)...) while((s32[]{:T(128)}, ...), condition=%wide.region_14.15_spmd.clone, body=%wide.region_9.14_spmd.clone.sunk | while | flops 29309844 | bytes 2495583 | solution.py:138
  281.0 0.6 dynamic_slice.78
  282.4 1.3 fusion.78
  283.7 0.3 fusion.79
  284.5 1.5 fusion.80
  286.0 1.1 fusion.83
  287.1 0.6 dynamic_slice.78
  288.5 1.3 fusion.78
  289.9 0.3 fusion.79
  290.6 1.5 fusion.80
  292.1 1.1 fusion.83
  293.2 0.6 dynamic_slice.78
  294.6 1.3 fusion.78
  296.0 0.3 fusion.79
  296.8 1.5 fusion.80
  298.2 1.1 fusion.83
  299.3 0.6 dynamic_slice.78
  300.8 1.3 fusion.78
  302.1 0.3 fusion.79
  302.9 1.5 fusion.80
  304.4 1.1 fusion.83
  305.5 0.6 dynamic_slice.78
  306.9 1.3 fusion.78
  308.2 0.3 fusion.79
  309.0 1.5 fusion.80
  310.5 1.1 fusion.83
  311.6 0.6 dynamic_slice.78
  313.0 1.3 fusion.78
  314.4 0.3 fusion.79
  315.1 1.5 fusion.80
  316.6 1.1 fusion.83
  317.9 1.2 convolution_convert_fusion
  319.2 0.7 iota_compare_fusion.1
  319.8 24.9 %reduce-scatter.2.cloned.1.call-done = bf16[40,768]{1,0:T(8,128)(2,1)} async-done(((bf16[40,3072]{1,0:T(8,128)(2,1)}), bf16[40,768]{1,0:T(8,128)(2,1)}) %reduce-scatter.2.cloned.1.call-update) | async-done | bytes 61456 | tf_op jit(solution)/shard_map/reduce_scatter | solution.py:141
  344.8 0.9 fusion.37
  345.8 7.4 %all-reduce = (f32[40]{0:T(128)S(1)}, f32[40]{0:T(128)S(1)}) all-reduce(f32[40]{0:T(128)S(1)} %get-tuple-element.105, f32[40]{0:T(128)S(1)} %get-tuple-element.104), channel_id=1, replica_groups=mesh['cfg'=2,'seq'=64,'tp'=4] {'tp'}, use_global_device_ids=true, to_apply=%region_19.20 | all-reduce | flops 80 | bytes 640 | tf_op jit(solution)/shard_map/psum | solution.py:147
  353.2 0.4 fusion.33
  353.6 13.4 %psum.23 = f32[40,64]{0,1:T(8,128)S(1)} all-reduce(f32[40,64]{0,1:T(8,128)S(1)} %fusion.33), channel_id=1, replica_groups=mesh['cfg'=2,'seq'=64,'tp'=4] {'tp'}, use_global_device_ids=true, to_apply=%region_20.21 | all-reduce | flops 2560 | bytes 20480 | tf_op jit(solution)/shard_map/psum | solution.py:159
  367.0 10.4 %collective-permute-start = (f32[40,64]{0,1:T(8,128)S(1)}, f32[40,64]{0,1:T(8,128)S(1)}, u32[]{:S(2)}, u32[]{:S(2)}) collective-permute-start(f32[40,64]{0,1:T(8,128)S(1)} %psum.23), channel_id=1, source_target_pairs={{0,256},{256,0},{1,257},{257,1},{2,258},{258,2},{3,259},{259,3},{4... | collective-permute-start | bytes 30728 | tf_op jit(solution)/shard_map/ppermute | solution.py:19
  378.0 1.4 fusion.60
  382.0 0.6 add_select_fusion.4
  (109 shorter events, 7.3 us)
Async XLA Ops:
  7.2 310.8 %copy-start = (bf16[384,3072]{1,0:T(8,128)(2,1)S(1)}, bf16[384,3072]{1,0:T(8,128)(2,1)}, u32[]{:S(2)}) copy-start(bf16[384,3072]{1,0:T(8,128)(2,1)} %param.25) | copy-start | bytes 7077892
  7.2 11.1 %copy-start.11 = (f32[64]{0:T(128)S(1)}, f32[64]{0:T(128)}, u32[]{:S(2)}) copy-start(f32[64]{0:T(128)} %param.31) | copy-start | bytes 772
  7.2 10.8 %copy-start.4 = (bf16[1,226,384]{2,1,0:T(8,128)(2,1)S(1)}, bf16[1,226,384]{2,1,0:T(8,128)(2,1)}, u32[]{:S(2)}) copy-start(bf16[1,226,384]{2,1,0:T(8,128)(2,1)} %param.23) | copy-start | bytes 520708
  7.2 140.0 %all-gather.5.cloned.1.call-start = ((), (), s32[]{:S(2)}) async-start(), calls=%async_computation.2 | async-start | bytes 1996800 | tf_op jit(solution)/shard_map/all_gather | solution.py:101
  7.9 273.0 %all-gather.7.cloned.1.call-start = ((), (), s32[]{:S(2)}) async-start(), calls=%async_computation.3 | async-start | bytes 1996800 | tf_op jit(solution)/shard_map/all_gather | solution.py:102
  8.7 336.1 %reduce-scatter.2.cloned.1.call-start = ((), (), s32[]{:S(2)}) async-start(), calls=%async_computation.1 | async-start | bytes 307200 | tf_op jit(solution)/shard_map/reduce_scatter | solution.py:141
  162.9 3.3 copy-start.1
  178.9 102.1 %copy-start.6 = (s32[64]{0:T(128)S(1)}, s32[64]{0:T(128)}, u32[]{:S(2)}) copy-start(s32[64]{0:T(128)} %param.32) | copy-start | bytes 772
  317.7 2.1 copy-start.10
  317.7 27.1 %copy-start.5 = (bf16[1,40,768]{2,1,0:T(8,128)(2,1)S(1)}, bf16[1,40,768]{2,1,0:T(8,128)(2,1)}, u32[]{:S(2)}) copy-start(bf16[1,40,768]{2,1,0:T(8,128)(2,1)} %param.19) | copy-start | bytes 184324
  317.7 27.0 %copy-start.8 = (f32[768]{0:T(1024)S(1)}, f32[768]{0:T(1024)}, u32[]{:S(2)}) copy-start(f32[768]{0:T(1024)} %param.26) | copy-start | bytes 9220
  317.7 35.5 %copy-start.3 = (f32[768,64]{0,1:T(8,128)S(1)}, f32[768,64]{0,1:T(8,128)}, u32[]{:S(2)}) copy-start(f32[768,64]{0,1:T(8,128)} %param.29) | copy-start | bytes 589828
  317.7 35.5 %copy-start.7 = (f32[768]{0:T(1024)S(1)}, f32[768]{0:T(1024)}, u32[]{:S(2)}) copy-start(f32[768]{0:T(1024)} %param.27) | copy-start | bytes 9220
  317.8 64.2 %copy-start.9 = (f32[40,8]{0,1:T(8,128)S(1)}, f32[40,8]{0,1:T(8,128)}, u32[]{:S(2)}) copy-start(f32[40,8]{0,1:T(8,128)} %param.33) | copy-start | bytes 3844
  345.7 36.9 %copy-start.2 = (bf16[40,768]{1,0:T(8,128)(2,1)}, bf16[40,768]{1,0:T(8,128)(2,1)S(1)}, u32[]{:S(2)}) copy-start(bf16[40,768]{1,0:T(8,128)(2,1)S(1)} %fusion.37) | copy-start | bytes 184324
  367.0 15.0 %collective-permute-start = (f32[40,64]{0,1:T(8,128)S(1)}, f32[40,64]{0,1:T(8,128)S(1)}, u32[]{:S(2)}, u32[]{:S(2)}) collective-permute-start(f32[40,64]{0,1:T(8,128)S(1)} %psum.23), channel_id=1, source_target_pairs={{0,256},{256,0},{1,257},{257,1},{2,258},{258,2},{3,259},{259,3},{4... | collective-permute-start | bytes 30728 | tf_op jit(solution)/shard_map/ppermute | solution.py:19
Sparse Core Ops, SparseCore 0:
  12.4 134.7 all-gather.4
  151.5 129.3 all-gather.6
  319.3 25.4 reduce-scatter.1
where the time goes:
time: 391 us; the launch traced here: 389 us
  waiting for transfers between devices  250 us (64%)
  other arithmetic  33.5 us (9%)
  matrix products  26.8 us (7%)
  local copies, waits for them, and re-layouts  25.8 us (7%)
  blocking collectives  20.8 us (5%)
  between operations  17.4 us (4%)
  starting transfers between devices  10.5 us (3%)
  loops' own time  4.14 us (1%)
    all_gather x1, waiting for transfers between devices, shards(): lax.all_gather(outgoing, 'seq', axis=0, tiled=True)  127 us
    all_gather x1, waiting for transfers between devices, shards(): lax.all_gather(values[0], 'seq', axis=0, tiled=True)  96.8 us
    reduce_scatter x1, waiting for transfers between devices, shards(): lax.psum_scatter(projected.astype(jnp.bfloat16), 'tp', scatter_dimension=...  24.9 us
    psum x1, blocking collectives, shards(): prediction = lax.psum(partial_pred, 'tp')  13.4 us
    ppermute x1, starting transfers between devices, partner_2(): lax.ppermute(shard, axis, [(i, i ^ 1 << distance) for i in range(lax.axis...  10.4 us
    dot_general x12, matrix products, last_dims(): lax.dot_general(left, right, (((1,), (1,)), ((), ())), preferred_element_...  9.89 us
    dot_general x6, matrix products, one_head(): jnp.dot(video_weights.astype(jnp.bfloat16), video_value_part, preferred_e...  8.91 us
  transfers between devices with their start and end apart: 4, of which 3 were waited for; matrix products, arithmetic and copies ran while one was open for 13% of the time, Pallas kernels for 0%

commit v1 on v0

v1 whole, which is shorter than its diff:
```python
import functools

import jax
import jax.numpy as jnp
import numpy as np
from jax import lax
from jax.experimental import pallas as pl
from jax.experimental.pallas import tpu as pltpu
from jax.sharding import PartitionSpec as P

NX = 4
NZ = 8
NY = 2
D = 3072
HEAD = 64
HP = 30
WP = 45
STRIDE = 20
ROWS = 40
TXT = 226
LANES = 128
PAIR = 2 * HEAD
PIECE = 8
STATS = 16

guide_scale = 6.0
head_eps = 1e-06
final_eps = 1e-05
LOW = -1e30
MESH = pl.DeviceIdType.MESH
F32 = jnp.float32
BF16 = jnp.bfloat16


def frequencies():
    def one(extent):
        return 1.0 / 10000.0 ** (np.arange(0, extent, 2, dtype=np.float32) / np.float32(extent))

    freq = np.concatenate([one(16), one(24), one(24)]).astype(np.float32)
    return np.repeat(freq, 2)[None, :].repeat(2, axis=0).reshape(1, PAIR)


def nt(left, right, precision=None):
    return lax.dot_general(
        left, right, (((1,), (1,)), ((), ())), precision=precision, preferred_element_type=F32
    )


def nn(left, right, precision=None):
    return lax.dot_general(
        left, right, (((1,), (0,)), ((), ())), precision=precision, preferred_element_type=F32
    )


def kernel(
    group,
    lengths,
    step_index,
    alphas,
    freq,
    q_gain,
    k_gain,
    stream_hbm,
    queries_hbm,
    keys_hbm,
    values_hbm,
    text_keys_hbm,
    text_values_hbm,
    weight_hbm,
    gate_hbm,
    shift_hbm,
    scale_hbm,
    proj_hbm,
    latents_hbm,
    hidden_out,
    latents_out,
    queries,
    keys,
    stream,
    text_keys,
    text_values,
    weight,
    gate,
    shift,
    scale,
    proj,
    latents,
    qbuf,
    kbuf,
    vbuf,
    osend,
    obuf,
    ssend,
    sbuf,
    rsend,
    rbuf,
    fsend,
    fbuf,
    load_sem,
    q_send,
    q_recv,
    k_send,
    k_recv,
    v_send,
    v_recv,
    o_send,
    o_recv,
    s_send,
    s_recv,
    r_send,
    r_recv,
    f_send,
    f_recv,
):
    n_kv = NX * NY
    total = 2 * group
    width = queries.shape[1]
    pairs = width // PAIR
    part = width * 2
    c = lax.axis_index("cfg")
    s = lax.axis_index("seq")
    t = lax.axis_index("tp")
    y = lax.rem(s, NY)
    z = lax.rem(lax.div(s, NY), NZ)
    x = lax.div(s, NY * NZ)
    rank = c * group + t

    def place(xx, zz, yy):
        return (c, (xx * NZ + zz) * NY + yy, t)

    z_of = [lax.rem(z + d, NZ) for d in range(1, NZ)]
    z_peers = [place(x, zz, y) for zz in z_of]
    x_of = [lax.rem(x + d, NX) for d in range(1, NX)]
    x_peers = [place(xx, z, y) for xx in x_of]
    y_peer = place(x, z, 1 - y)
    t_of = [lax.rem(t + d, group) for d in range(1, group)]
    t_peers = [(c, s, tt) for tt in t_of]
    g_of = [lax.rem(rank + d, total) for d in range(1, total)]
    g_peers = [(lax.div(g, group), s, lax.rem(g, group)) for g in g_of]

    barrier = pltpu.get_barrier_semaphore()
    everyone = z_peers + x_peers + ([y_peer] if NY > 1 else []) + g_peers
    for peer in everyone:
        pl.semaphore_signal(barrier, inc=1, device_id=peer, device_id_type=MESH)

    own = x * NY + y
    other = x * NY + (1 - y)

    loads = []

    def load(src, dst):
        copy = pltpu.make_async_copy(src, dst, load_sem.at[len(loads)])
        copy.start()
        loads.append(copy)
        return copy

    load_k = load(keys_hbm.at[0], keys)
    load_q = load(queries_hbm.at[0], queries)
    load_v = load(values_hbm.at[0], vbuf.at[own])
    load_tk = load(text_keys_hbm.at[0], text_keys)
    load_tv = load(text_values_hbm.at[0], text_values)
    load_w = [load(weight_hbm.at[:, pl.ds(j * part, part)], weight.at[j]) for j in range(group)]
    load_rest = [
        load(stream_hbm.at[0], stream),
        load(gate_hbm, gate),
        load(shift_hbm, shift),
        load(scale_hbm, scale),
        load(proj_hbm, proj),
        load(latents_hbm, latents),
    ]

    lane = lax.broadcasted_iota(jnp.int32, (1, PAIR), 1)
    within_head = lax.rem(lane, HEAD)
    is_even = lax.rem(lane, 2) == 0
    first_head = lane < HEAD
    own_start = jnp.int32(0)
    for b in range(NX * NZ * NY):
        own_start = own_start + jnp.where(b < s, lengths[b], 0)
    own_count = lengths[s]
    row = lax.broadcasted_iota(jnp.int32, (ROWS, PAIR), 0)
    live_rows = row < own_count
    position = (row + own_start).astype(F32)
    frame = jnp.floor((position + 0.5) * (1.0 / (HP * WP)))
    line = jnp.floor((position + 0.5) * (1.0 / WP))
    across = position - line * WP
    height = line - frame * HP
    coord = jnp.where(within_head < 16, frame, jnp.where(within_head < 40, height, across))
    angle = coord * freq[...]
    cos_table = jnp.cos(angle)
    sin_table = jnp.sin(angle)
    sin_table = jnp.where(is_even, -sin_table, sin_table)

    r_io = lax.broadcasted_iota(jnp.int32, (PAIR, PAIR), 0)
    c_io = lax.broadcasted_iota(jnp.int32, (PAIR, PAIR), 1)
    mean_matrix = jnp.where((r_io < HEAD) == (c_io < HEAD), 1.0 / HEAD, 0.0)
    mean_matrix_low = mean_matrix.astype(BF16)
    gain_q = jnp.concatenate([q_gain[...], q_gain[...]], axis=1)
    gain_k = jnp.concatenate([k_gain[...], k_gain[...]], axis=1)

    def head_norm(field, gain):
        centre = field.astype(F32) - nn(field, mean_matrix_low)
        spread = nn(centre * centre, mean_matrix, lax.Precision.HIGHEST)
        return centre * lax.rsqrt(spread + head_eps) * gain

    def rotate(field):
        swapped = jnp.where(
            is_even, pltpu.roll(field, PAIR - 1, 1), pltpu.roll(field, 1, 1)
        )
        return field * cos_table + swapped * sin_table

    def pair_slice(p):
        return pl.ds(p * PAIR, PAIR)

    load_k.wait()
    for p in range(pairs):
        made = rotate(head_norm(keys[:, pair_slice(p)], gain_k)).astype(BF16)
        kbuf[own, :, pair_slice(p)] = made
    load_q.wait()
    for p in range(pairs):
        made = rotate(head_norm(queries[:, pair_slice(p)], gain_q)).astype(BF16)
        qbuf[z, :, pair_slice(p)] = made

    pl.semaphore_wait(barrier, len(everyone))

    sent = []

    def send(src, dst, send_sem, recv_sem, peer):
        copy = pltpu.make_async_remote_copy(
            src_ref=src,
            dst_ref=dst,
            send_sem=send_sem,
            recv_sem=recv_sem,
            device_id=peer,
            device_id_type=MESH,
        )
        copy.start()
        sent.append(copy)

    def arrive(ref, send_sem, recv_sem, peer):
        pltpu.make_async_remote_copy(
            src_ref=ref,
            dst_ref=ref,
            send_sem=send_sem,
            recv_sem=recv_sem,
            device_id=peer,
            device_id_type=MESH,
        ).wait_recv()

    if NY > 1:
        send(values_hbm.at[0], vbuf.at[own], v_send.at[0], v_recv.at[own], y_peer)
        send(kbuf.at[own], kbuf.at[own], k_send.at[0], k_recv.at[own], y_peer)
    order_z = sorted(range(1, NZ), key=lambda d: -min(d, NZ - d))
    for d in order_z:
        send(qbuf.at[z], qbuf.at[z], q_send.at[d], q_recv.at[z], z_peers[d - 1])
    for d in range(1, NX):
        send(values_hbm.at[0], vbuf.at[own], v_send.at[d], v_recv.at[own], x_peers[d - 1])
        send(kbuf.at[own], kbuf.at[own], k_send.at[d], k_recv.at[own], x_peers[d - 1])

    load_tk.wait()
    load_tv.wait()
    text_mixed = []
    lane_row = lax.broadcasted_iota(jnp.int32, (ROWS, LANES), 1)
    text_stat = jnp.where(lax.rem(lane_row, 8) >= 6, 1.0, 0.0)
    for p in range(pairs):
        made = head_norm(text_keys[:, pair_slice(p)], gain_k)
        query_part = qbuf[z, :, pair_slice(p)]
        value_part = text_values[:, pair_slice(p)]
        outs = []
        for which in range(2):
            chosen = first_head if which == 0 else jnp.logical_not(first_head)
            key_part = jnp.where(chosen, made, 0.0).astype(BF16)
            scores = nt(query_part, key_part) * 0.125
            top = jnp.max(scores, axis=1, keepdims=True)
            weights = jnp.exp(scores - top)
            count = jnp.sum(weights, axis=1, keepdims=True)
            outs.append(nn(weights.astype(BF16), value_part))
            head = 2 * p + which
            text_stat = jnp.where(lane_row == head, top, text_stat)
            text_stat = jnp.where(lane_row == 8 + head, count, text_stat)
        text_mixed.append(jnp.where(first_head, outs[0], outs[1]))
    below = jnp.zeros((LANES - ROWS, LANES), F32)
    text_stat = jnp.concatenate([text_stat, below], axis=0).T[0:STATS]

    if NY > 1:
        arrive(vbuf.at[other], v_send.at[0], v_recv.at[other], y_peer)
        for d in range(1, NX):
            send(vbuf.at[other], vbuf.at[other], v_send.at[NX - 1 + d], v_recv.at[other], x_peers[d - 1])
        arrive(kbuf.at[other], k_send.at[0], k_recv.at[other], y_peer)
        for d in range(1, NX):
            send(kbuf.at[other], kbuf.at[other], k_send.at[NX - 1 + d], k_recv.at[other], x_peers[d - 1])
    for d in range(1, NZ):
        zz = z_of[d - 1]
        arrive(qbuf.at[zz], q_send.at[d], q_recv.at[zz], z_peers[d - 1])
    load_v.wait()
    for yy in [y, 1 - y][:NY]:
        for d in range(1, NX):
            slot = x_of[d - 1] * NY + yy
            arrive(kbuf.at[slot], k_send.at[d], k_recv.at[slot], x_peers[d - 1])
            arrive(vbuf.at[slot], v_send.at[d], v_recv.at[slot], x_peers[d - 1])

    keys_all = n_kv * ROWS
    keys_up = -(-keys_all // LANES) * LANES
    key_lane = lax.broadcasted_iota(jnp.int32, (1, keys_up), 1)
    live_key = key_lane < 0
    for j in range(n_kv):
        held = lengths[((j // NY) * NZ + z) * NY + j % NY]
        live_key = live_key | ((key_lane >= j * ROWS) & (key_lane < j * ROWS + held))
    spare = [jnp.zeros((keys_up - keys_all, PAIR), F32)] if keys_up > keys_all else []
    stat = jnp.where(lax.rem(lane_row, 8) >= 6, 1.0, 0.0)
    for p in range(pairs):
        query_part = jnp.concatenate(
            [qbuf[j, :, pair_slice(p)].astype(F32) for j in range(NZ)], axis=0
        ).astype(BF16)
        key_part = jnp.concatenate(
            [kbuf[j, :, pair_slice(p)].astype(F32) for j in range(n_kv)] + spare, axis=0
        )
        value_part = jnp.concatenate(
            [vbuf[j, :, pair_slice(p)].astype(F32) for j in range(n_kv)] + spare, axis=0
        ).astype(BF16)
        outs = []
        for which in range(2):
            chosen = first_head if which == 0 else jnp.logical_not(first_head)
            scores = nt(query_part, jnp.where(chosen, key_part, 0.0).astype(BF16)) * 0.125
            scores = jnp.where(live_key, scores, LOW)
            top = jnp.max(scores, axis=1, keepdims=True)
            weights = jnp.exp(scores - top)
            count = jnp.sum(weights, axis=1, keepdims=True)
            outs.append(nn(weights.astype(BF16), value_part))
            head = 2 * p + which
            for j in range(NZ):
                rows = slice(j * ROWS, (j + 1) * ROWS)
                stat = jnp.where(lane_row == j * STATS + head, top[rows], stat)
                stat = jnp.where(lane_row == j * STATS + 8 + head, count[rows], stat)
        mixed = jnp.where(first_head, outs[0], outs[1])
        for j in range(NZ):
            osend[j, :, pair_slice(p)] = mixed[j * ROWS : (j + 1) * ROWS].astype(BF16)
    stat = jnp.concatenate([stat, below], axis=0).T
    for j in range(NZ):
        ssend[j] = stat[j * STATS : (j + 1) * STATS]
    for d in order_z:
        zz = z_of[d - 1]
        send(ssend.at[zz], sbuf.at[z], s_send.at[d], s_recv.at[z], z_peers[d - 1])
        send(osend.at[zz], obuf.at[z], o_send.at[d], o_recv.at[z], z_peers[d - 1])

    for d in range(1, NZ):
        zz = z_of[d - 1]
        arrive(sbuf.at[zz], s_send.at[d], s_recv.at[zz], z_peers[d - 1])
        arrive(obuf.at[zz], o_send.at[d], o_recv.at[zz], z_peers[d - 1])
    sources = [jnp.int32(0) + z] + z_of
    stats = [ssend[z]] + [sbuf[zz] for zz in z_of] + [text_stat]
    top = stats[0][0:8]
    for one in stats[1:]:
        top = jnp.maximum(top, one[0:8])
    factors = [jnp.exp(one[0:8] - top) for one in stats]
    whole = factors[0] * stats[0][8:16]
    for factor, one in zip(factors[1:], stats[1:]):
        whole = whole + factor * one[8:16]
    share = jnp.concatenate(
        [factor / whole for factor in factors]
        + [jnp.zeros((LANES - 8 * len(factors), LANES), F32)],
        axis=0,
    ).T
    attended = []
    for p in range(pairs):
        pieces = [osend[z, :, pair_slice(p)]] + [obuf[zz, :, pair_slice(p)] for zz in z_of]
        pieces = [piece.astype(F32) for piece in pieces] + [text_mixed[p]]
        joined = jnp.zeros((ROWS, PAIR), F32)
        for j, piece in enumerate(pieces):
            lower = share[0:ROWS, 8 * j + 2 * p : 8 * j + 2 * p + 1]
            upper = share[0:ROWS, 8 * j + 2 * p + 1 : 8 * j + 2 * p + 2]
            joined = joined + piece * jnp.where(first_head, lower, upper)
        attended.append(joined.astype(BF16))
    attended = jnp.concatenate(attended, axis=1)

    for copy in load_w:
        copy.wait()
    for d in sorted(range(1, group), reverse=True):
        tt = t_of[d - 1]
        rsend[d - 1] = nn(attended, weight[tt]).astype(BF16)
        send(rsend.at[d - 1], rbuf.at[t], r_send.at[d], r_recv.at[t], t_peers[d - 1])
    summed = nn(attended, weight[t])
    for copy in load_rest:
        copy.wait()
    lifted = 1.0 + scale[...]
    for d in range(1, group):
        tt = t_of[d - 1]
        arrive(rbuf.at[tt], r_send.at[d], r_recv.at[tt], t_peers[d - 1])
        summed = summed + rbuf[tt].astype(F32)
    hidden = stream[...].astype(F32) + gate[...] * summed
    hidden = jnp.where(live_rows[:, 0:1], hidden, 0.0).astype(BF16)
    hidden_out[0] = hidden
    widened = hidden.astype(F32)

    channels = total * PIECE
    tall = ROWS + 8
    extra = jnp.concatenate([lifted, shift[...], jnp.zeros((6, part), F32)], axis=0)
    stacked = jnp.concatenate([widened * lifted, extra], axis=0)
    flipped = nt(proj[...], stacked, lax.Precision.HIGHEST)
    row_sum = nt(jnp.ones((8, part), BF16), hidden)
    row_square = nt(jnp.ones((8, part), F32), widened * widened, lax.Precision.HIGHEST)
    flipped = jnp.concatenate([flipped, jnp.zeros((channels, LANES - tall), F32)], axis=1)
    sums = jnp.where(lax.broadcasted_iota(jnp.int32, (8, ROWS), 0) == 0, row_sum, row_square)
    sums = jnp.concatenate([sums, jnp.zeros((8, LANES - ROWS), F32)], axis=1)
    for g in range(total):
        fsend[g, 0:8, :] = flipped[g * PIECE : (g + 1) * PIECE]
        fsend[g, 8:16, :] = sums
    for d in range(1, total):
        g = g_of[d - 1]
        send(fsend.at[g], fbuf.at[rank], f_send.at[d], f_recv.at[rank], g_peers[d - 1])
    for d in range(1, total):
        g = g_of[d - 1]
        arrive(fbuf.at[g], f_send.at[d], f_recv.at[g], g_peers[d - 1])

    def prediction(half):
        gathered = jnp.zeros((16, LANES), F32)
        for tt in range(group):
            g = half * group + tt
            gathered = gathered + jnp.where(rank == g, fsend[g], fbuf[g])
        mean = gathered[8:9] / D
        square = gathered[9:10] / D
        base = gathered[0:8]
        ratio = lax.rsqrt(square - mean * mean + final_eps)
        lifted_sum = base[:, ROWS : ROWS + 1]
        shift_sum = base[:, ROWS + 1 : ROWS + 2]
        return ratio * (base - mean * lifted_sum) + shift_sum

    conditioned = prediction(0)
    unconditioned = prediction(1)
    guided = unconditioned + guide_scale * (conditioned - unconditioned)
    guided = guided[:, 0:ROWS]
    step = step_index[0]
    current = jnp.zeros((1, ROWS), F32) + alphas[step]
    earlier = jnp.zeros((1, ROWS), F32) + alphas[jnp.maximum(step - STRIDE, 0)]
    root_now = jnp.sqrt(current)
    rest_now = jnp.sqrt(1.0 - current)
    held = latents[...]
    clean = root_now * held - rest_now * guided
    noise = root_now * guided + rest_now * held
    stepped = jnp.sqrt(earlier) * clean + jnp.sqrt(1.0 - earlier) * noise
    token = lax.broadcasted_iota(jnp.int32, (1, ROWS), 1)
    latents_out[...] = jnp.where(token < own_count, stepped, 0.0)

    for copy in sent:
        copy.wait_send()


def shards(
    group,
    stream,
    queries,
    keys,
    values,
    text_keys,
    text_values,
    out_weight,
    gate,
    shift,
    scale,
    proj_weight,
    q_gain,
    k_gain,
    lengths,
    latents,
    alphas,
    step_index,
):
    width = queries.shape[2]
    part = stream.shape[2]
    n_kv = NX * NY
    total = 2 * group
    freq = jnp.asarray(frequencies())
    smem = pl.BlockSpec(memory_space=pltpu.SMEM)
    vmem = pl.BlockSpec(memory_space=pltpu.VMEM)
    anywhere = pl.BlockSpec(memory_space=pl.ANY)
    dma = pltpu.SemaphoreType.DMA
    hidden_out, latents_out = pl.pallas_call(
        functools.partial(kernel, group),
        name="step",
        out_shape=(
            jax.ShapeDtypeStruct((1, ROWS, part), BF16),
            jax.ShapeDtypeStruct((PIECE, ROWS), F32),
        ),
        in_specs=[smem, smem, smem, vmem, vmem, vmem] + [anywhere] * 12,
        out_specs=(vmem, vmem),
        scratch_shapes=[
            pltpu.VMEM((ROWS, width), BF16),
            pltpu.VMEM((ROWS, width), BF16),
            pltpu.VMEM((ROWS, part), BF16),
            pltpu.VMEM((TXT, width), BF16),
            pltpu.VMEM((TXT, width), BF16),
            pltpu.VMEM((group, width, part), BF16),
            pltpu.VMEM((1, part), F32),
            pltpu.VMEM((1, part), F32),
            pltpu.VMEM((1, part), F32),
            pltpu.VMEM((total * PIECE, part), F32),
            pltpu.VMEM((PIECE, ROWS), F32),
            pltpu.VMEM((NZ, ROWS, width), BF16),
            pltpu.VMEM((n_kv, ROWS, width), BF16),
            pltpu.VMEM((n_kv, ROWS, width), BF16),
            pltpu.VMEM((NZ, ROWS, width), BF16),
            pltpu.VMEM((NZ, ROWS, width), BF16),
            pltpu.VMEM((NZ, STATS, LANES), F32),
            pltpu.VMEM((NZ, STATS, LANES), F32),
            pltpu.VMEM((max(group - 1, 1), ROWS, part), BF16),
            pltpu.VMEM((group, ROWS, part), BF16),
            pltpu.VMEM((total, 16, LANES), F32),
            pltpu.VMEM((total, 16, LANES), F32),
            dma((11 + group,)),
            dma((NZ,)),
            dma((NZ,)),
            dma((2 * NX,)),
            dma((n_kv,)),
            dma((2 * NX,)),
            dma((n_kv,)),
            dma((NZ,)),
            dma((NZ,)),
            dma((NZ,)),
            dma((NZ,)),
            dma((group,)),
            dma((group,)),
            dma((total,)),
            dma((total,)),
        ],
        compiler_params=pltpu.CompilerParams(collective_id=0, has_side_effects=True),
    )(
        lengths,
        step_index,
        alphas,
        freq,
        q_gain.reshape(1, HEAD),
        k_gain.reshape(1, HEAD),
        stream,
        queries,
        keys,
        values,
        text_keys,
        text_values,
        out_weight,
        gate.reshape(1, part),
        shift.reshape(1, part),
        scale.reshape(1, part),
        proj_weight.T,
        latents.T,
    )
    return hidden_out, latents_out.T


def solution(mesh):
    return jax.shard_map(
        functools.partial(shards, mesh.shape["tp"]),
        mesh=mesh,
        in_specs=(
            P("cfg", "seq", "tp"),
            P("cfg", "seq", "tp"),
            P("cfg", "seq", "tp"),
            P("cfg", "seq", "tp"),
            P("cfg", None, "tp"),
            P("cfg", None, "tp"),
            P("tp", None),
            P("tp"),
            P("tp"),
            P("tp"),
            P("tp", None),
            P(),
            P(),
            P(),
            P("seq", ("cfg", "tp")),
            P(),
            P(),
        ),
        out_specs=(P("cfg", "seq", "tp"), P("seq", ("cfg", "tp"))),
        check_vma=False,
    )
```

time: 391 us -> 55.9 us (0.14)
  waiting for transfers between devices: 250 us -> 0 us
  Pallas kernels: 0 us -> 47.7 us
  other arithmetic: 33.5 us -> 0 us
  matrix products: 26.8 us -> 0 us
  blocking collectives: 20.8 us -> 0 us
  local copies, waits for them, and re-layouts: 25.8 us -> 6.55 us
  between operations: 17.4 us -> 1.29 us
  starting transfers between devices: 10.5 us -> 0 us
  loops' own time: 4.14 us -> 0 us
    all_gather x2 -> x0, waiting for transfers between devices: 224 us -> none  [the longest x1 127 us: shards(): lax.all_gather(outgoing, 'seq', axis=0, tiled=True)]
    pallas_call x0 -> x1, Pallas kernels: none -> 47.7 us  [shards(): pl.pallas_call(functools.partial(kernel, group), name='step', out_shape=(...]
    dot_general x26 -> x0, matrix products: 26.8 us -> none  [the longest x12 9.89 us: last_dims(): lax.dot_general(left, right, (((1,), (1,)), ((), ())), preferred_element_...]
    reduce_scatter x1 -> x0, waiting for transfers between devices: 24.9 us -> none  [shards(): lax.psum_scatter(projected.astype(jnp.bfloat16), 'tp', scatter_dimension=...]
    psum x2 -> x0, blocking collectives: 20.8 us -> none  [the longest x1 13.4 us: shards(): prediction = lax.psum(partial_pred, 'tp')]
    another operation x6 -> x0, other arithmetic: 11.6 us -> none  [the longest x2 6 us: rotate_pairs(): jnp.stack([first * cos_part - second * sin_part, second * cos_part + firs...]
    ppermute x1 -> x0, starting transfers between devices: 10.4 us -> none  [partner_2(): lax.ppermute(shard, axis, [(i, i ^ 1 << distance) for i in range(lax.axis...]
    reduce_sum x20 -> x0, other arithmetic: 9.78 us -> none  [the longest x3 3.11 us: head_norm(): spread = jnp.mean(centre * centre, axis=-1, keepdims=True)]
  transfers between devices with their start and end apart: 4 -> 0, of which waited for: 3 -> 0; matrix products, arithmetic and copies ran while one was open for 13% -> 0% of each run, Pallas kernels for 0% -> 0%
where the time goes in v1:
time: 55.9 us; the launch traced here: 55.5 us
  Pallas kernels  47.7 us (85%)
  local copies, waits for them, and re-layouts  6.55 us (12%)
  between operations  1.29 us (2%)
    pallas_call x1, Pallas kernels, shards(): pl.pallas_call(functools.partial(kernel, group), name='step', out_shape=(...  47.7 us
    unnamed x2, local copies, waits for them, and re-layouts  2.73 us
    reshape x1, local copies, waits for them, and re-layouts, shards(): scale.reshape(1, part)  1.28 us
    reshape x1, local copies, waits for them, and re-layouts, shards(): gate.reshape(1, part)  1.27 us
    reshape x1, local copies, waits for them, and re-layouts, shards(): shift.reshape(1, part)  1.27 us

profile of v1, /device:TPU:1, one launch (start us, length us, event | category | flops | bytes accessed | tf_op | source)
XLA Modules:
  0.0 55.5 jit_solution(3563892766734078893)
XLA Ops:
  1.3 1.3 %reshape.21.gate_hbm = f32[1,768]{1,0:T(1,128)} reshape(f32[768]{0:T(1024)} %param.25) | data formatting | bytes 6144 | tf_op jit(solution)/shard_map/reshape | solution.py:539
  2.5 1.3 %reshape.22.shift_hbm = f32[1,768]{1,0:T(1,128)} reshape(f32[768]{0:T(1024)} %param.26) | data formatting | bytes 6144 | tf_op jit(solution)/shard_map/reshape | solution.py:540
  3.8 1.3 %reshape.23.scale_hbm = f32[1,768]{1,0:T(1,128)} reshape(f32[768]{0:T(1024)} %param.27) | data formatting | bytes 6144 | tf_op jit(solution)/shard_map/reshape | solution.py:541
  5.1 47.7 %step.1 = (bf16[1,40,768]{2,1,0:T(8,128)(2,1)}, f32[8,40]{1,0:T(8,128)}) custom-call(s32[64]{0:T(128)} %lengths.1, s32[1]{0:T(128)S(6)} %copy.22.step_index, f32[1000]{0:T(1024)} %alphas.1, f32[1,128]{1,0:T(1,128)} %constant.2.clone.freq, f32[1,64]{1,0:T(1,128)} %bitcast.8, f32[1,64]{1,0:T(1,128)} %bitcast.9, bf16[1,40,768]{2,1,0:T(8,128)(2,1)} %stream_hbm.1, ...), custom_call_target="tpu_custom_call" | custom-call | tf_op jit(solution)/shard_map/step/pallas_call | solution.py:476
  52.8 1.5 %copy.23 = bf16[1,40,768]{2,1,0:T(8,128)(2,1)} copy(bf16[1,40,768]{2,1,0:T(8,128)(2,1)} %get-tuple-element.8) | data formatting | bytes 122880
  54.2 1.3 %copy.24 = f32[40,8]{0,1:T(8,128)} copy(f32[40,8]{0,1:T(8,128)} %bitcast.7) | data formatting | bytes 2560

commit v2 on v1

--- a/solution.py
+++ b/solution.py
@@ -54,12 +54,12 @@
 
 def kernel(
     group,
-    lengths,
-    step_index,
-    alphas,
-    freq,
-    q_gain,
-    k_gain,
+    lengths_hbm,
+    step_index_hbm,
+    alphas_hbm,
+    freq_hbm,
+    q_gain_hbm,
+    k_gain_hbm,
     stream_hbm,
     queries_hbm,
     keys_hbm,
@@ -74,6 +74,12 @@
     latents_hbm,
     hidden_out,
     latents_out,
+    lengths,
+    step_index,
+    alphas,
+    freq,
+    q_gain,
+    k_gain,
     queries,
     keys,
     stream,
@@ -154,7 +160,9 @@
         loads.append(copy)
         return copy
 
+    load_lengths = load(lengths_hbm, lengths)
     load_k = load(keys_hbm.at[0], keys)
+    load_small = [load(freq_hbm, freq), load(q_gain_hbm, q_gain), load(k_gain_hbm, k_gain)]
     load_q = load(queries_hbm.at[0], queries)
     load_v = load(values_hbm.at[0], vbuf.at[own])
     load_tk = load(text_keys_hbm.at[0], text_keys)
@@ -162,6 +170,8 @@
     load_w = [load(weight_hbm.at[:, pl.ds(j * part, part)], weight.at[j]) for j in range(group)]
     load_rest = [
         load(stream_hbm.at[0], stream),
+        load(step_index_hbm, step_index),
+        load(alphas_hbm, alphas),
         load(gate_hbm, gate),
         load(shift_hbm, shift),
         load(scale_hbm, scale),
@@ -169,6 +179,9 @@
         load(latents_hbm, latents),
     ]
 
+    load_lengths.wait()
+    for copy in load_small:
+        copy.wait()
     lane = lax.broadcasted_iota(jnp.int32, (1, PAIR), 1)
     within_head = lax.rem(lane, HEAD)
     is_even = lax.rem(lane, 2) == 0
@@ -194,12 +207,17 @@
     c_io = lax.broadcasted_iota(jnp.int32, (PAIR, PAIR), 1)
     mean_matrix = jnp.where((r_io < HEAD) == (c_io < HEAD), 1.0 / HEAD, 0.0)
     mean_matrix_low = mean_matrix.astype(BF16)
-    gain_q = jnp.concatenate([q_gain[...], q_gain[...]], axis=1)
-    gain_k = jnp.concatenate([k_gain[...], k_gain[...]], axis=1)
+    gain_q = q_gain[...].reshape(1, HEAD)
+    gain_q = jnp.concatenate([gain_q, gain_q], axis=1)
+    gain_k = k_gain[...].reshape(1, HEAD)
+    gain_k = jnp.concatenate([gain_k, gain_k], axis=1)
 
     def head_norm(field, gain):
         centre = field.astype(F32) - nn(field, mean_matrix_low)
-        spread = nn(centre * centre, mean_matrix, lax.Precision.HIGHEST)
+        square = centre * centre
+        high = square.astype(BF16)
+        low = (square - high.astype(F32)).astype(BF16)
+        spread = nn(high, mean_matrix_low) + nn(low, mean_matrix_low)
         return centre * lax.rsqrt(spread + head_eps) * gain
 
     def rotate(field):
@@ -215,11 +233,6 @@
     for p in range(pairs):
         made = rotate(head_norm(keys[:, pair_slice(p)], gain_k)).astype(BF16)
         kbuf[own, :, pair_slice(p)] = made
-    load_q.wait()
-    for p in range(pairs):
-        made = rotate(head_norm(queries[:, pair_slice(p)], gain_q)).astype(BF16)
-        qbuf[z, :, pair_slice(p)] = made
-
     pl.semaphore_wait(barrier, len(everyone))
 
     sent = []
@@ -249,12 +262,18 @@
     if NY > 1:
         send(values_hbm.at[0], vbuf.at[own], v_send.at[0], v_recv.at[own], y_peer)
         send(kbuf.at[own], kbuf.at[own], k_send.at[0], k_recv.at[own], y_peer)
-    order_z = sorted(range(1, NZ), key=lambda d: -min(d, NZ - d))
-    for d in order_z:
-        send(qbuf.at[z], qbuf.at[z], q_send.at[d], q_recv.at[z], z_peers[d - 1])
     for d in range(1, NX):
         send(values_hbm.at[0], vbuf.at[own], v_send.at[d], v_recv.at[own], x_peers[d - 1])
         send(kbuf.at[own], kbuf.at[own], k_send.at[d], k_recv.at[own], x_peers[d - 1])
+
+    order_z = sorted(range(1, NZ), key=lambda d: -min(d, NZ - d))
+    load_q.wait()
+    for p in range(pairs):
+        made = rotate(head_norm(queries[:, pair_slice(p)], gain_q)).astype(BF16)
+        qbuf[z, :, pair_slice(p)] = made
+
+    for d in order_z:
+        send(qbuf.at[z], qbuf.at[z], q_send.at[d], q_recv.at[z], z_peers[d - 1])
 
     load_tk.wait()
     load_tv.wait()
@@ -291,33 +310,38 @@
     for d in range(1, NZ):
         zz = z_of[d - 1]
         arrive(qbuf.at[zz], q_send.at[d], q_recv.at[zz], z_peers[d - 1])
+    for d in range(1, NX):
+        slot = x_of[d - 1] * NY + y
+        arrive(kbuf.at[slot], k_send.at[d], k_recv.at[slot], x_peers[d - 1])
+        arrive(vbuf.at[slot], v_send.at[d], v_recv.at[slot], x_peers[d - 1])
     load_v.wait()
-    for yy in [y, 1 - y][:NY]:
-        for d in range(1, NX):
-            slot = x_of[d - 1] * NY + yy
-            arrive(kbuf.at[slot], k_send.at[d], k_recv.at[slot], x_peers[d - 1])
-            arrive(vbuf.at[slot], v_send.at[d], v_recv.at[slot], x_peers[d - 1])
-
-    keys_all = n_kv * ROWS
+
+    keys_all = NX * ROWS
     keys_up = -(-keys_all // LANES) * LANES
     key_lane = lax.broadcasted_iota(jnp.int32, (1, keys_up), 1)
-    live_key = key_lane < 0
-    for j in range(n_kv):
-        held = lengths[((j // NY) * NZ + z) * NY + j % NY]
-        live_key = live_key | ((key_lane >= j * ROWS) & (key_lane < j * ROWS + held))
     spare = [jnp.zeros((keys_up - keys_all, PAIR), F32)] if keys_up > keys_all else []
-    stat = jnp.where(lax.rem(lane_row, 8) >= 6, 1.0, 0.0)
+
+    def gather(buf, p, yy):
+        blocks = [buf[j * NY + yy, :, pair_slice(p)].astype(F32) for j in range(NX)]
+        return jnp.concatenate(blocks + spare, axis=0)
+
+    def live_of(yy):
+        live = key_lane < 0
+        for j in range(NX):
+            held = lengths[(j * NZ + z) * NY + yy]
+            live = live | ((key_lane >= j * ROWS) & (key_lane < j * ROWS + held))
+        return live
+
+    query_parts = []
+    partials = []
+    live_key = live_of(y)
     for p in range(pairs):
         query_part = jnp.concatenate(
             [qbuf[j, :, pair_slice(p)].astype(F32) for j in range(NZ)], axis=0
         ).astype(BF16)
-        key_part = jnp.concatenate(
-            [kbuf[j, :, pair_slice(p)].astype(F32) for j in range(n_kv)] + spare, axis=0
-        )
-        value_part = jnp.concatenate(
-            [vbuf[j, :, pair_slice(p)].astype(F32) for j in range(n_kv)] + spare, axis=0
-        ).astype(BF16)
-        outs = []
+        query_parts.append(query_part)
+        key_part = gather(kbuf, p, y)
+        value_part = gather(vbuf, p, y).astype(BF16)
         for which in range(2):
             chosen = first_head if which == 0 else jnp.logical_not(first_head)
             scores = nt(query_part, jnp.where(chosen, key_part, 0.0).astype(BF16)) * 0.125
@@ -325,36 +349,65 @@
             top = jnp.max(scores, axis=1, keepdims=True)
             weights = jnp.exp(scores - top)
             count = jnp.sum(weights, axis=1, keepdims=True)
-            outs.append(nn(weights.astype(BF16), value_part))
+            partials.append((top, count, nn(weights.astype(BF16), value_part)))
+
+    if NY > 1:
+        for d in range(1, NX):
+            slot = x_of[d - 1] * NY + 1 - y
+            arrive(kbuf.at[slot], k_send.at[d], k_recv.at[slot], x_peers[d - 1])
+            arrive(vbuf.at[slot], v_send.at[d], v_recv.at[slot], x_peers[d - 1])
+    stat = jnp.where(lax.rem(lane_row, 8) >= 6, 1.0, 0.0)
+    live_key = live_of(1 - y)
+    for p in range(pairs):
+        if NY > 1:
+            key_part = gather(kbuf, p, 1 - y)
+            value_part = gather(vbuf, p, 1 - y).astype(BF16)
+        outs = []
+        for which in range(2):
             head = 2 * p + which
+            top, count, out = partials[head]
+            if NY > 1:
+                chosen = first_head if which == 0 else jnp.logical_not(first_head)
+                scores = nt(query_parts[p], jnp.where(chosen, key_part, 0.0).astype(BF16)) * 0.125
+                scores = jnp.where(live_key, scores, LOW)
+                before = top
+                top = jnp.maximum(before, jnp.max(scores, axis=1, keepdims=True))
+                fade = jnp.exp(before - top)
+                weights = jnp.exp(scores - top)
+                count = count * fade + jnp.sum(weights, axis=1, keepdims=True)
+                out = out * fade + nn(weights.astype(BF16), value_part)
+            outs.append(out)
             for j in range(NZ):
                 rows = slice(j * ROWS, (j + 1) * ROWS)
                 stat = jnp.where(lane_row == j * STATS + head, top[rows], stat)
                 stat = jnp.where(lane_row == j * STATS + 8 + head, count[rows], stat)
         mixed = jnp.where(first_head, outs[0], outs[1])
         for j in range(NZ):
-            osend[j, :, pair_slice(p)] = mixed[j * ROWS : (j + 1) * ROWS].astype(BF16)
-    stat = jnp.concatenate([stat, below], axis=0).T
-    for j in range(NZ):
-        ssend[j] = stat[j * STATS : (j + 1) * STATS]
-    for d in order_z:
-        zz = z_of[d - 1]
-        send(ssend.at[zz], sbuf.at[z], s_send.at[d], s_recv.at[z], z_peers[d - 1])
-        send(osend.at[zz], obuf.at[z], o_send.at[d], o_recv.at[z], z_peers[d - 1])
+            osend[p, j] = mixed[j * ROWS : (j + 1) * ROWS].astype(BF16)
+        if p == pairs - 1:
+            flat = jnp.concatenate([stat, below], axis=0).T
+            for j in range(NZ):
+                tops = flat[j * STATS : j * STATS + 8]
+                counts = flat[j * STATS + 8 : j * STATS + 16]
+                ssend[j] = tops + pltpu.roll(counts, HEAD, 1)
+            for d in order_z:
+                zz = z_of[d - 1]
+                send(ssend.at[zz], sbuf.at[z], s_send.at[d], s_recv.at[z], z_peers[d - 1])
+        for d in order_z:
+            zz = z_of[d - 1]
+            send(osend.at[p, zz], obuf.at[p, z], o_send.at[p, d], o_recv.at[p, z], z_peers[d - 1])
 
     for d in range(1, NZ):
         zz = z_of[d - 1]
         arrive(sbuf.at[zz], s_send.at[d], s_recv.at[zz], z_peers[d - 1])
-        arrive(obuf.at[zz], o_send.at[d], o_recv.at[zz], z_peers[d - 1])
-    sources = [jnp.int32(0) + z] + z_of
-    stats = [ssend[z]] + [sbuf[zz] for zz in z_of] + [text_stat]
-    top = stats[0][0:8]
-    for one in stats[1:]:
-        top = jnp.maximum(top, one[0:8])
-    factors = [jnp.exp(one[0:8] - top) for one in stats]
-    whole = factors[0] * stats[0][8:16]
-    for factor, one in zip(factors[1:], stats[1:]):
-        whole = whole + factor * one[8:16]
+        for p in range(pairs):
+            arrive(obuf.at[p, zz], o_send.at[p, d], o_recv.at[p, zz], z_peers[d - 1])
+    tiles = [ssend[z]] + [sbuf[zz] for zz in z_of]
+    tops = tiles + [text_stat[0:8]]
+    counts = [pltpu.roll(tile, HEAD, 1) for tile in tiles] + [text_stat[8:16]]
+    top = functools.reduce(jnp.maximum, tops)
+    factors = [jnp.exp(one - top) for one in tops]
+    whole = sum(factor * count for factor, count in zip(factors, counts))
     share = jnp.concatenate(
         [factor / whole for factor in factors]
         + [jnp.zeros((LANES - 8 * len(factors), LANES), F32)],
@@ -362,7 +415,7 @@
     ).T
     attended = []
     for p in range(pairs):
-        pieces = [osend[z, :, pair_slice(p)]] + [obuf[zz, :, pair_slice(p)] for zz in z_of]
+        pieces = [osend[p, z]] + [obuf[p, zz] for zz in z_of]
         pieces = [piece.astype(F32) for piece in pieces] + [text_mixed[p]]
         joined = jnp.zeros((ROWS, PAIR), F32)
         for j, piece in enumerate(pieces):
@@ -381,29 +434,28 @@
     summed = nn(attended, weight[t])
     for copy in load_rest:
         copy.wait()
-    lifted = 1.0 + scale[...]
+    lifted = 1.0 + scale[...].reshape(1, part)
     for d in range(1, group):
         tt = t_of[d - 1]
         arrive(rbuf.at[tt], r_send.at[d], r_recv.at[tt], t_peers[d - 1])
         summed = summed + rbuf[tt].astype(F32)
-    hidden = stream[...].astype(F32) + gate[...] * summed
+    hidden = stream[...].astype(F32) + gate[...].reshape(1, part) * summed
     hidden = jnp.where(live_rows[:, 0:1], hidden, 0.0).astype(BF16)
     hidden_out[0] = hidden
     widened = hidden.astype(F32)
 
     channels = total * PIECE
     tall = ROWS + 8
-    extra = jnp.concatenate([lifted, shift[...], jnp.zeros((6, part), F32)], axis=0)
+    extra = jnp.concatenate([lifted, shift[...].reshape(1, part), jnp.zeros((6, part), F32)], axis=0)
     stacked = jnp.concatenate([widened * lifted, extra], axis=0)
     flipped = nt(proj[...], stacked, lax.Precision.HIGHEST)
     row_sum = nt(jnp.ones((8, part), BF16), hidden)
     row_square = nt(jnp.ones((8, part), F32), widened * widened, lax.Precision.HIGHEST)
-    flipped = jnp.concatenate([flipped, jnp.zeros((channels, LANES - tall), F32)], axis=1)
+    flipped = jnp.concatenate([flipped, jnp.zeros((channels, HEAD - tall), F32)], axis=1)
     sums = jnp.where(lax.broadcasted_iota(jnp.int32, (8, ROWS), 0) == 0, row_sum, row_square)
-    sums = jnp.concatenate([sums, jnp.zeros((8, LANES - ROWS), F32)], axis=1)
+    sums = jnp.concatenate([sums, jnp.zeros((8, HEAD - ROWS), F32)], axis=1)
     for g in range(total):
-        fsend[g, 0:8, :] = flipped[g * PIECE : (g + 1) * PIECE]
-        fsend[g, 8:16, :] = sums
+        fsend[g] = jnp.concatenate([flipped[g * PIECE : (g + 1) * PIECE], sums], axis=1)
     for d in range(1, total):
         g = g_of[d - 1]
         send(fsend.at[g], fbuf.at[rank], f_send.at[d], f_recv.at[rank], g_peers[d - 1])
@@ -412,13 +464,14 @@
         arrive(fbuf.at[g], f_send.at[d], f_recv.at[g], g_peers[d - 1])
 
     def prediction(half):
-        gathered = jnp.zeros((16, LANES), F32)
+        gathered = jnp.zeros((8, LANES), F32)
         for tt in range(group):
             g = half * group + tt
             gathered = gathered + jnp.where(rank == g, fsend[g], fbuf[g])
-        mean = gathered[8:9] / D
-        square = gathered[9:10] / D
-        base = gathered[0:8]
+        sums = pltpu.roll(gathered, HEAD, 1)
+        mean = sums[0:1] / D
+        square = sums[1:2] / D
+        base = gathered
         ratio = lax.rsqrt(square - mean * mean + final_eps)
         lifted_sum = base[:, ROWS : ROWS + 1]
         shift_sum = base[:, ROWS + 1 : ROWS + 2]
@@ -442,6 +495,34 @@
 
     for copy in sent:
         copy.wait_send()
+
+
+def finish_kernel(hidden, latents, hidden_out, latents_out, sem):
+    copies = [
+        pltpu.make_async_copy(hidden, hidden_out, sem.at[0]),
+        pltpu.make_async_copy(latents, latents_out, sem.at[1]),
+    ]
+    for copy in copies:
+        copy.start()
+    for copy in copies:
+        copy.wait()
+
+
+def finish(hidden, latents):
+    vmem = pl.BlockSpec(memory_space=pltpu.VMEM)
+    anywhere = pl.BlockSpec(memory_space=pl.ANY)
+    hidden, latents = pl.pallas_call(
+        finish_kernel,
+        name="finish",
+        out_shape=(
+            jax.ShapeDtypeStruct(hidden.shape, hidden.dtype),
+            jax.ShapeDtypeStruct(latents.shape, latents.dtype),
+        ),
+        in_specs=[vmem, vmem],
+        out_specs=(anywhere, anywhere),
+        scratch_shapes=[pltpu.SemaphoreType.DMA((2,))],
+    )(hidden, latents)
+    return hidden, latents.T
 
 
 def shards(
@@ -469,7 +550,6 @@
     n_kv = NX * NY
     total = 2 * group
     freq = jnp.asarray(frequencies())
-    smem = pl.BlockSpec(memory_space=pltpu.SMEM)
     vmem = pl.BlockSpec(memory_space=pltpu.VMEM)
     anywhere = pl.BlockSpec(memory_space=pl.ANY)
     dma = pltpu.SemaphoreType.DMA
@@ -480,40 +560,46 @@
             jax.ShapeDtypeStruct((1, ROWS, part), BF16),
             jax.ShapeDtypeStruct((PIECE, ROWS), F32),
         ),
-        in_specs=[smem, smem, smem, vmem, vmem, vmem] + [anywhere] * 12,
+        in_specs=[anywhere] * 18,
         out_specs=(vmem, vmem),
         scratch_shapes=[
+            pltpu.SMEM((NX * NZ * NY,), jnp.int32),
+            pltpu.SMEM((1,), jnp.int32),
+            pltpu.SMEM((alphas.shape[0],), F32),
+            pltpu.VMEM((1, PAIR), F32),
+            pltpu.VMEM((HEAD,), F32),
+            pltpu.VMEM((HEAD,), F32),
             pltpu.VMEM((ROWS, width), BF16),
             pltpu.VMEM((ROWS, width), BF16),
             pltpu.VMEM((ROWS, part), BF16),
             pltpu.VMEM((TXT, width), BF16),
             pltpu.VMEM((TXT, width), BF16),
             pltpu.VMEM((group, width, part), BF16),
-            pltpu.VMEM((1, part), F32),
-            pltpu.VMEM((1, part), F32),
-            pltpu.VMEM((1, part), F32),
+            pltpu.VMEM((part,), F32),
+            pltpu.VMEM((part,), F32),
+            pltpu.VMEM((part,), F32),
             pltpu.VMEM((total * PIECE, part), F32),
             pltpu.VMEM((PIECE, ROWS), F32),
             pltpu.VMEM((NZ, ROWS, width), BF16),
             pltpu.VMEM((n_kv, ROWS, width), BF16),
             pltpu.VMEM((n_kv, ROWS, width), BF16),
-            pltpu.VMEM((NZ, ROWS, width), BF16),
-            pltpu.VMEM((NZ, ROWS, width), BF16),
-            pltpu.VMEM((NZ, STATS, LANES), F32),
-            pltpu.VMEM((NZ, STATS, LANES), F32),
+            pltpu.VMEM((width // PAIR, NZ, ROWS, PAIR), BF16),
+            pltpu.VMEM((width // PAIR, NZ, ROWS, PAIR), BF16),
+            pltpu.VMEM((NZ, 8, LANES), F32),
+            pltpu.VMEM((NZ, 8, LANES), F32),
             pltpu.VMEM((max(group - 1, 1), ROWS, part), BF16),
             pltpu.VMEM((group, ROWS, part), BF16),
-            pltpu.VMEM((total, 16, LANES), F32),
-            pltpu.VMEM((total, 16, LANES), F32),
-            dma((11 + group,)),
+            pltpu.VMEM((total, 8, LANES), F32),
+            pltpu.VMEM((total, 8, LANES), F32),
+            dma((17 + group,)),
             dma((NZ,)),
             dma((NZ,)),
             dma((2 * NX,)),
             dma((n_kv,)),
             dma((2 * NX,)),
             dma((n_kv,)),
-            dma((NZ,)),
-            dma((NZ,)),
+            dma((width // PAIR, NZ)),
+            dma((width // PAIR, NZ)),
             dma((NZ,)),
             dma((NZ,)),
             dma((group,)),
@@ -527,8 +613,8 @@
         step_index,
         alphas,
         freq,
-        q_gain.reshape(1, HEAD),
-        k_gain.reshape(1, HEAD),
+        q_gain,
+        k_gain,
         stream,
         queries,
         keys,
@@ -536,13 +622,13 @@
         text_keys,
         text_values,
         out_weight,
-        gate.reshape(1, part),
-        shift.reshape(1, part),
-        scale.reshape(1, part),
+        gate,
+        shift,
+        scale,
         proj_weight.T,
         latents.T,
     )
-    return hidden_out, latents_out.T
+    return finish(hidden_out, latents_out)
 
 
 def solution(mesh):

time: 55.9 us -> 47.5 us (0.85)
  local copies, waits for them, and re-layouts: 6.55 us -> 0 us
  Pallas kernels: 47.7 us -> 46.1 us
    reshape x3 -> x0, local copies, waits for them, and re-layouts: 3.82 us -> none  [the longest x1 1.28 us: shards(): scale.reshape(1, part)]
    pallas_call x1, Pallas kernels: 47.7 us -> 44.6 us  [shards(): pl.pallas_call(functools.partial(kernel, group), name='step', out_shape=(...]
    unnamed x2 -> x0, local copies, waits for them, and re-layouts: 2.73 us -> none
    pallas_call x0 -> x1, Pallas kernels: none -> 1.47 us  [finish(): pl.pallas_call(finish_kernel, name='finish', out_shape=(jax.ShapeDtypeStr...]
where the time goes in v2:
time: 47.5 us; the launch traced here: 47.3 us
  Pallas kernels  46.1 us (97%)
  between operations  1.29 us (3%)
    pallas_call x1, Pallas kernels, shards(): pl.pallas_call(functools.partial(kernel, group), name='step', out_shape=(...  44.6 us
    pallas_call x1, Pallas kernels, finish(): pl.pallas_call(finish_kernel, name='finish', out_shape=(jax.ShapeDtypeStr...  1.47 us

profile of v2, /device:TPU:1, one launch (start us, length us, event | category | flops | bytes accessed | tf_op | source)
XLA Modules:
  0.0 47.3 jit_solution(1415002510071210222)
XLA Ops:
  1.3 44.6 %step.1 = (bf16[1,40,768]{2,1,0:T(8,128)(2,1)}, f32[8,40]{1,0:T(8,128)}) custom-call(s32[64]{0:T(128)} %lengths_hbm.1, s32[1]{0:T(128)S(6)} %copy.20.step_index_hbm, f32[1000]{0:T(1024)} %alphas_hbm.1, f32[1,128]{1,0:T(1,128)} %constant.2.clone.freq_hbm, f32[64]{0:T(128)} %q_gain_hbm.1, f32[64]{0:T(128)} %k_gain_hbm.1, bf16[1,40,768]{2,1,0:T(8,128)(2,1)} %stream_hbm.1, ...), custom_call_target="tpu_custom_call" | custom-call | tf_op jit(solution)/shard_map/step/pallas_call | solution.py:556
  45.9 1.5 %finish.1 = (bf16[1,40,768]{2,1,0:T(8,128)(2,1)}, f32[8,40]{1,0:T(8,128)}) custom-call(bf16[1,40,768]{2,1,0:T(8,128)(2,1)} %get-tuple-element.6.hidden, f32[8,40]{1,0:T(8,128)} %get-tuple-element.7.latents), custom_call_target="tpu_custom_call" | custom-call | tf_op jit(solution)/shard_map/finish/pallas_call | solution.py:514

commit v3 on v2

--- a/solution.py
+++ b/solution.py
@@ -27,6 +27,7 @@
 head_eps = 1e-06
 final_eps = 1e-05
 LOW = -1e30
+QUERY, NEAR, OTHER_V, OTHER_K, FAR, STAT, OUT, PART, LAST = range(9)
 MESH = pl.DeviceIdType.MESH
 F32 = jnp.float32
 BF16 = jnp.bfloat16
@@ -103,20 +104,8 @@
     fsend,
     fbuf,
     load_sem,
-    q_send,
-    q_recv,
-    k_send,
-    k_recv,
-    v_send,
-    v_recv,
-    o_send,
-    o_recv,
-    s_send,
-    s_recv,
-    r_send,
-    r_recv,
-    f_send,
-    f_recv,
+    send_sem,
+    recv_sem,
 ):
     n_kv = NX * NY
     total = 2 * group
@@ -139,7 +128,7 @@
     x_of = [lax.rem(x + d, NX) for d in range(1, NX)]
     x_peers = [place(xx, z, y) for xx in x_of]
     y_peer = place(x, z, 1 - y)
-    t_of = [lax.rem(t + d, group) for d in range(1, group)]
+    t_of = [t + 1 - 2 * lax.rem(t, 2), lax.rem(t + 2, group), group - 1 - t][: group - 1]
     t_peers = [(c, s, tt) for tt in t_of]
     g_of = [lax.rem(rank + d, total) for d in range(1, total)]
     g_peers = [(lax.div(g, group), s, lax.rem(g, group)) for g in g_of]
@@ -152,34 +141,34 @@
     own = x * NY + y
     other = x * NY + (1 - y)
 
-    loads = []
-
-    def load(src, dst):
-        copy = pltpu.make_async_copy(src, dst, load_sem.at[len(loads)])
+    def load(src, dst, which):
+        copy = pltpu.make_async_copy(src, dst, load_sem.at[which])
         copy.start()
-        loads.append(copy)
         return copy
 
-    load_lengths = load(lengths_hbm, lengths)
-    load_k = load(keys_hbm.at[0], keys)
-    load_small = [load(freq_hbm, freq), load(q_gain_hbm, q_gain), load(k_gain_hbm, k_gain)]
-    load_q = load(queries_hbm.at[0], queries)
-    load_v = load(values_hbm.at[0], vbuf.at[own])
-    load_tk = load(text_keys_hbm.at[0], text_keys)
-    load_tv = load(text_values_hbm.at[0], text_values)
-    load_w = [load(weight_hbm.at[:, pl.ds(j * part, part)], weight.at[j]) for j in range(group)]
+    load_small = [
+        load(lengths_hbm, lengths, 0),
+        load(freq_hbm, freq, 1),
+        load(q_gain_hbm, q_gain, 2),
+        load(k_gain_hbm, k_gain, 3),
+    ]
+    load_k = load(keys_hbm.at[0], keys, 4)
+    load_q = load(queries_hbm.at[0], queries, 5)
+    load_v = load(values_hbm.at[0], vbuf.at[own], 6)
+    load_text = [load(text_keys_hbm.at[0], text_keys, 7), load(text_values_hbm.at[0], text_values, 8)]
+    for j in range(group):
+        load(weight_hbm.at[:, pl.ds(j * part, part)], weight.at[j], 9)
     load_rest = [
-        load(stream_hbm.at[0], stream),
-        load(step_index_hbm, step_index),
-        load(alphas_hbm, alphas),
-        load(gate_hbm, gate),
-        load(shift_hbm, shift),
-        load(scale_hbm, scale),
-        load(proj_hbm, proj),
-        load(latents_hbm, latents),
+        load(step_index_hbm, step_index, 10),
+        load(alphas_hbm, alphas, 11),
+        load(stream_hbm.at[0], stream, 12),
+        load(gate_hbm, gate, 13),
+        load(shift_hbm, shift, 14),
+        load(scale_hbm, scale, 15),
+        load(proj_hbm, proj, 16),
+        load(latents_hbm, latents, 17),
     ]
 
-    load_lengths.wait()
     for copy in load_small:
         copy.wait()
     lane = lax.broadcasted_iota(jnp.int32, (1, PAIR), 1)
@@ -235,36 +224,36 @@
         kbuf[own, :, pair_slice(p)] = made
     pl.semaphore_wait(barrier, len(everyone))
 
-    sent = []
-
-    def send(src, dst, send_sem, recv_sem, peer):
+    def send(src, dst, kind, which, peer):
         copy = pltpu.make_async_remote_copy(
             src_ref=src,
             dst_ref=dst,
-            send_sem=send_sem,
-            recv_sem=recv_sem,
+            send_sem=send_sem.at[kind],
+            recv_sem=recv_sem.at[which],
             device_id=peer,
             device_id_type=MESH,
         )
         copy.start()
-        sent.append(copy)
-
-    def arrive(ref, send_sem, recv_sem, peer):
-        pltpu.make_async_remote_copy(
+
+    def whole_copy(ref, kind, which):
+        return pltpu.make_async_remote_copy(
             src_ref=ref,
             dst_ref=ref,
-            send_sem=send_sem,
-            recv_sem=recv_sem,
-            device_id=peer,
+            send_sem=send_sem.at[kind],
+            recv_sem=recv_sem.at[which],
+            device_id=g_peers[0],
             device_id_type=MESH,
-        ).wait_recv()
+        )
+
+    def arrive(ref, which):
+        whole_copy(ref, 0, which).wait_recv()
 
     if NY > 1:
-        send(values_hbm.at[0], vbuf.at[own], v_send.at[0], v_recv.at[own], y_peer)
-        send(kbuf.at[own], kbuf.at[own], k_send.at[0], k_recv.at[own], y_peer)
+        send(values_hbm.at[0], vbuf.at[own], 1, OTHER_V, y_peer)
+        send(kbuf.at[own], kbuf.at[own], 0, OTHER_K, y_peer)
     for d in range(1, NX):
-        send(values_hbm.at[0], vbuf.at[own], v_send.at[d], v_recv.at[own], x_peers[d - 1])
-        send(kbuf.at[own], kbuf.at[own], k_send.at[d], k_recv.at[own], x_peers[d - 1])
+        send(values_hbm.at[0], vbuf.at[own], 1, NEAR, x_peers[d - 1])
+        send(kbuf.at[own], kbuf.at[own], 0, NEAR, x_peers[d - 1])
 
     order_z = sorted(range(1, NZ), key=lambda d: -min(d, NZ - d))
     load_q.wait()
@@ -273,10 +262,10 @@
         qbuf[z, :, pair_slice(p)] = made
 
     for d in order_z:
-        send(qbuf.at[z], qbuf.at[z], q_send.at[d], q_recv.at[z], z_peers[d - 1])
-
-    load_tk.wait()
-    load_tv.wait()
+        send(qbuf.at[z], qbuf.at[z], 2, QUERY, z_peers[d - 1])
+
+    for copy in load_text:
+        copy.wait()
     text_mixed = []
     lane_row = lax.broadcasted_iota(jnp.int32, (ROWS, LANES), 1)
     text_stat = jnp.where(lax.rem(lane_row, 8) >= 6, 1.0, 0.0)
@@ -301,107 +290,107 @@
     text_stat = jnp.concatenate([text_stat, below], axis=0).T[0:STATS]
 
     if NY > 1:
-        arrive(vbuf.at[other], v_send.at[0], v_recv.at[other], y_peer)
+        arrive(vbuf.at[other], OTHER_V)
         for d in range(1, NX):
-            send(vbuf.at[other], vbuf.at[other], v_send.at[NX - 1 + d], v_recv.at[other], x_peers[d - 1])
-        arrive(kbuf.at[other], k_send.at[0], k_recv.at[other], y_peer)
+            send(vbuf.at[other], vbuf.at[other], 1, FAR, x_peers[d - 1])
+        arrive(kbuf.at[other], OTHER_K)
         for d in range(1, NX):
-            send(kbuf.at[other], kbuf.at[other], k_send.at[NX - 1 + d], k_recv.at[other], x_peers[d - 1])
-    for d in range(1, NZ):
-        zz = z_of[d - 1]
-        arrive(qbuf.at[zz], q_send.at[d], q_recv.at[zz], z_peers[d - 1])
-    for d in range(1, NX):
-        slot = x_of[d - 1] * NY + y
-        arrive(kbuf.at[slot], k_send.at[d], k_recv.at[slot], x_peers[d - 1])
-        arrive(vbuf.at[slot], v_send.at[d], v_recv.at[slot], x_peers[d - 1])
+            send(kbuf.at[other], kbuf.at[other], 0, FAR, x_peers[d - 1])
+    arrive(qbuf.at[pl.ds(0, NZ - 1)], QUERY)
+    arrive(kbuf.at[pl.ds(0, 2 * (NX - 1))], NEAR)
     load_v.wait()
 
-    keys_all = NX * ROWS
-    keys_up = -(-keys_all // LANES) * LANES
-    key_lane = lax.broadcasted_iota(jnp.int32, (1, keys_up), 1)
-    spare = [jnp.zeros((keys_up - keys_all, PAIR), F32)] if keys_up > keys_all else []
+    n_keys = NX * ROWS
+    n_queries = NZ * ROWS
+    q_up = -(-n_queries // LANES) * LANES
+    slot_row = lax.broadcasted_iota(jnp.int32, (ROWS, 1), 0)
 
     def gather(buf, p, yy):
         blocks = [buf[j * NY + yy, :, pair_slice(p)].astype(F32) for j in range(NX)]
-        return jnp.concatenate(blocks + spare, axis=0)
+        return jnp.concatenate(blocks, axis=0)
 
     def live_of(yy):
-        live = key_lane < 0
-        for j in range(NX):
-            held = lengths[(j * NZ + z) * NY + yy]
-            live = live | ((key_lane >= j * ROWS) & (key_lane < j * ROWS + held))
-        return live
+        pieces = [
+            jnp.where(slot_row < lengths[(j * NZ + z) * NY + yy], 0.0, LOW) for j in range(NX)
+        ]
+        return jnp.concatenate(pieces + pieces, axis=0)
+
+    def score(p, yy, live):
+        key_part = gather(kbuf, p, yy)
+        both = jnp.concatenate(
+            [jnp.where(first_head, key_part, 0.0), jnp.where(first_head, 0.0, key_part)], axis=0
+        ).astype(BF16)
+        found = jnp.where(live < 0.0, LOW, nt(both, query_parts[p]) * 0.125)
+        turned = gather(vbuf, p, yy).T.astype(BF16)
+        return [
+            (found[w * n_keys : (w + 1) * n_keys], turned[w * HEAD : (w + 1) * HEAD])
+            for w in range(2)
+        ]
 
     query_parts = []
     partials = []
-    live_key = live_of(y)
+    live = live_of(y)
     for p in range(pairs):
-        query_part = jnp.concatenate(
-            [qbuf[j, :, pair_slice(p)].astype(F32) for j in range(NZ)], axis=0
-        ).astype(BF16)
-        query_parts.append(query_part)
-        key_part = gather(kbuf, p, y)
-        value_part = gather(vbuf, p, y).astype(BF16)
-        for which in range(2):
-            chosen = first_head if which == 0 else jnp.logical_not(first_head)
-            scores = nt(query_part, jnp.where(chosen, key_part, 0.0).astype(BF16)) * 0.125
-            scores = jnp.where(live_key, scores, LOW)
-            top = jnp.max(scores, axis=1, keepdims=True)
+        query_parts.append(
+            jnp.concatenate(
+                [qbuf[j, :, pair_slice(p)].astype(F32) for j in range(NZ)], axis=0
+            ).astype(BF16)
+        )
+    near = [score(p, y, live) for p in range(pairs)]
+    for p in range(pairs):
+        for scores, turned in near[p]:
+            top = jnp.max(scores, axis=0, keepdims=True)
             weights = jnp.exp(scores - top)
-            count = jnp.sum(weights, axis=1, keepdims=True)
-            partials.append((top, count, nn(weights.astype(BF16), value_part)))
+            count = jnp.sum(weights, axis=0, keepdims=True)
+            partials.append((top, count, nn(turned, weights.astype(BF16))))
 
     if NY > 1:
-        for d in range(1, NX):
-            slot = x_of[d - 1] * NY + 1 - y
-            arrive(kbuf.at[slot], k_send.at[d], k_recv.at[slot], x_peers[d - 1])
-            arrive(vbuf.at[slot], v_send.at[d], v_recv.at[slot], x_peers[d - 1])
-    stat = jnp.where(lax.rem(lane_row, 8) >= 6, 1.0, 0.0)
-    live_key = live_of(1 - y)
+        arrive(kbuf.at[pl.ds(0, 2 * (NX - 1))], FAR)
+    live = live_of(1 - y)
+    stat_row = lax.broadcasted_iota(jnp.int32, (8, q_up), 0)
+    tops = jnp.zeros((8, q_up), F32)
+    counts = jnp.ones((8, q_up), F32)
+    lane_tile = lax.broadcasted_iota(jnp.int32, (8, LANES), 1)
+
+    def widen(line):
+        if q_up == n_queries:
+            return line
+        return jnp.concatenate([line, jnp.zeros((line.shape[0], q_up - n_queries), F32)], axis=1)
+
+    far = [score(p, 1 - y, live) for p in range(pairs)] if NY > 1 else None
     for p in range(pairs):
-        if NY > 1:
-            key_part = gather(kbuf, p, 1 - y)
-            value_part = gather(vbuf, p, 1 - y).astype(BF16)
         outs = []
         for which in range(2):
             head = 2 * p + which
             top, count, out = partials[head]
             if NY > 1:
-                chosen = first_head if which == 0 else jnp.logical_not(first_head)
-                scores = nt(query_parts[p], jnp.where(chosen, key_part, 0.0).astype(BF16)) * 0.125
-                scores = jnp.where(live_key, scores, LOW)
+                scores, turned = far[p][which]
                 before = top
-                top = jnp.maximum(before, jnp.max(scores, axis=1, keepdims=True))
+                top = jnp.maximum(before, jnp.max(scores, axis=0, keepdims=True))
                 fade = jnp.exp(before - top)
                 weights = jnp.exp(scores - top)
-                count = count * fade + jnp.sum(weights, axis=1, keepdims=True)
-                out = out * fade + nn(weights.astype(BF16), value_part)
+                count = count * fade + jnp.sum(weights, axis=0, keepdims=True)
+                out = out * fade + nn(turned, weights.astype(BF16))
             outs.append(out)
-            for j in range(NZ):
-                rows = slice(j * ROWS, (j + 1) * ROWS)
-                stat = jnp.where(lane_row == j * STATS + head, top[rows], stat)
-                stat = jnp.where(lane_row == j * STATS + 8 + head, count[rows], stat)
-        mixed = jnp.where(first_head, outs[0], outs[1])
+            tops = jnp.where(stat_row == head, widen(top), tops)
+            counts = jnp.where(stat_row == head, widen(count), counts)
+        mixed = widen(jnp.concatenate(outs, axis=0)).T
         for j in range(NZ):
             osend[p, j] = mixed[j * ROWS : (j + 1) * ROWS].astype(BF16)
         if p == pairs - 1:
-            flat = jnp.concatenate([stat, below], axis=0).T
             for j in range(NZ):
-                tops = flat[j * STATS : j * STATS + 8]
-                counts = flat[j * STATS + 8 : j * STATS + 16]
-                ssend[j] = tops + pltpu.roll(counts, HEAD, 1)
+                left = pltpu.roll(tops, (q_up - j * ROWS) % q_up, 1)[:, 0:LANES]
+                right = pltpu.roll(counts, (q_up + HEAD - j * ROWS) % q_up, 1)[:, 0:LANES]
+                ssend[j] = jnp.where(lane_tile < HEAD, left, right)
             for d in order_z:
                 zz = z_of[d - 1]
-                send(ssend.at[zz], sbuf.at[z], s_send.at[d], s_recv.at[z], z_peers[d - 1])
+                send(ssend.at[zz], sbuf.at[z], 3, STAT, z_peers[d - 1])
         for d in order_z:
             zz = z_of[d - 1]
-            send(osend.at[p, zz], obuf.at[p, z], o_send.at[p, d], o_recv.at[p, z], z_peers[d - 1])
-
-    for d in range(1, NZ):
-        zz = z_of[d - 1]
-        arrive(sbuf.at[zz], s_send.at[d], s_recv.at[zz], z_peers[d - 1])
-        for p in range(pairs):
-            arrive(obuf.at[p, zz], o_send.at[p, d], o_recv.at[p, zz], z_peers[d - 1])
+            send(osend.at[p, zz], obuf.at[p, z], 4, OUT, z_peers[d - 1])
+
+    arrive(sbuf.at[pl.ds(0, NZ - 1)], STAT)
+    arrive(obuf.at[:, pl.ds(0, NZ - 1)], OUT)
     tiles = [ssend[z]] + [sbuf[zz] for zz in z_of]
     tops = tiles + [text_stat[0:8]]
     counts = [pltpu.roll(tile, HEAD, 1) for tile in tiles] + [text_stat[8:16]]
@@ -425,19 +414,17 @@
         attended.append(joined.astype(BF16))
     attended = jnp.concatenate(attended, axis=1)
 
-    for copy in load_w:
-        copy.wait()
+    pltpu.make_async_copy(weight, weight, load_sem.at[9]).wait()
     for d in sorted(range(1, group), reverse=True):
         tt = t_of[d - 1]
         rsend[d - 1] = nn(attended, weight[tt]).astype(BF16)
-        send(rsend.at[d - 1], rbuf.at[t], r_send.at[d], r_recv.at[t], t_peers[d - 1])
+        send(rsend.at[d - 1], rbuf.at[t], 5, PART, t_peers[d - 1])
     summed = nn(attended, weight[t])
     for copy in load_rest:
         copy.wait()
     lifted = 1.0 + scale[...].reshape(1, part)
-    for d in range(1, group):
-        tt = t_of[d - 1]
-        arrive(rbuf.at[tt], r_send.at[d], r_recv.at[tt], t_peers[d - 1])
+    arrive(rbuf.at[pl.ds(0, group - 1)], PART)
+    for tt in t_of:
         summed = summed + rbuf[tt].astype(F32)
     hidden = stream[...].astype(F32) + gate[...].reshape(1, part) * summed
     hidden = jnp.where(live_rows[:, 0:1], hidden, 0.0).astype(BF16)
@@ -458,10 +445,8 @@
         fsend[g] = jnp.concatenate([flipped[g * PIECE : (g + 1) * PIECE], sums], axis=1)
     for d in range(1, total):
         g = g_of[d - 1]
-        send(fsend.at[g], fbuf.at[rank], f_send.at[d], f_recv.at[rank], g_peers[d - 1])
-    for d in range(1, total):
-        g = g_of[d - 1]
-        arrive(fbuf.at[g], f_send.at[d], f_recv.at[g], g_peers[d - 1])
+        send(fsend.at[g], fbuf.at[rank], 6, LAST, g_peers[d - 1])
+    arrive(fbuf.at[pl.ds(0, total - 1)], LAST)
 
     def prediction(half):
         gathered = jnp.zeros((8, LANES), F32)
@@ -481,7 +466,7 @@
     unconditioned = prediction(1)
     guided = unconditioned + guide_scale * (conditioned - unconditioned)
     guided = guided[:, 0:ROWS]
-    step = step_index[0]
+    step = step_index[0, 0]
     current = jnp.zeros((1, ROWS), F32) + alphas[step]
     earlier = jnp.zeros((1, ROWS), F32) + alphas[jnp.maximum(step - STRIDE, 0)]
     root_now = jnp.sqrt(current)
@@ -493,8 +478,19 @@
     token = lax.broadcasted_iota(jnp.int32, (1, ROWS), 1)
     latents_out[...] = jnp.where(token < own_count, stepped, 0.0)
 
-    for copy in sent:
-        copy.wait_send()
+    n_block = NX - 1 + (NX if NY > 1 else 0)
+    for kind, ref in enumerate(
+        [
+            kbuf.at[pl.ds(0, n_block)],
+            vbuf.at[pl.ds(0, n_block)],
+            qbuf.at[pl.ds(0, NZ - 1)],
+            sbuf.at[pl.ds(0, NZ - 1)],
+            obuf.at[:, pl.ds(0, NZ - 1)],
+            rbuf.at[pl.ds(0, group - 1)],
+            fbuf.at[pl.ds(0, total - 1)],
+        ]
+    ):
+        whole_copy(ref, kind, 0).wait_send()
 
 
 def finish_kernel(hidden, latents, hidden_out, latents_out, sem):
@@ -521,7 +517,10 @@
         in_specs=[vmem, vmem],
         out_specs=(anywhere, anywhere),
         scratch_shapes=[pltpu.SemaphoreType.DMA((2,))],
-    )(hidden, latents)
+    )(
+        pltpu.with_memory_space_constraint(hidden, pltpu.VMEM),
+        pltpu.with_memory_space_constraint(latents, pltpu.VMEM),
+    )
     return hidden, latents.T
 
 
@@ -557,14 +556,14 @@
         functools.partial(kernel, group),
         name="step",
         out_shape=(
-            jax.ShapeDtypeStruct((1, ROWS, part), BF16),
-            jax.ShapeDtypeStruct((PIECE, ROWS), F32),
+            pltpu.VMEM((1, ROWS, part), BF16),
+            pltpu.VMEM((PIECE, ROWS), F32),
         ),
         in_specs=[anywhere] * 18,
         out_specs=(vmem, vmem),
         scratch_shapes=[
             pltpu.SMEM((NX * NZ * NY,), jnp.int32),
-            pltpu.SMEM((1,), jnp.int32),
+            pltpu.SMEM((1, 1), jnp.int32),
             pltpu.SMEM((alphas.shape[0],), F32),
             pltpu.VMEM((1, PAIR), F32),
             pltpu.VMEM((HEAD,), F32),
@@ -591,26 +590,14 @@
             pltpu.VMEM((group, ROWS, part), BF16),
             pltpu.VMEM((total, 8, LANES), F32),
             pltpu.VMEM((total, 8, LANES), F32),
-            dma((17 + group,)),
-            dma((NZ,)),
-            dma((NZ,)),
-            dma((2 * NX,)),
-            dma((n_kv,)),
-            dma((2 * NX,)),
-            dma((n_kv,)),
-            dma((width // PAIR, NZ)),
-            dma((width // PAIR, NZ)),
-            dma((NZ,)),
-            dma((NZ,)),
-            dma((group,)),
-            dma((group,)),
-            dma((total,)),
-            dma((total,)),
+            dma((18,)),
+            dma((7,)),
+            dma((9,)),
         ],
         compiler_params=pltpu.CompilerParams(collective_id=0, has_side_effects=True),
     )(
         lengths,
-        step_index,
+        step_index.reshape(1, 1),
         alphas,
         freq,
         q_gain,

time: 47.5 us -> 45.2 us (0.952)
  Pallas kernels: 46.1 us -> 43.8 us
    pallas_call x1, Pallas kernels: 44.6 us -> 43.1 us  [shards(): pl.pallas_call(functools.partial(kernel, group), name='step', out_shape=(...]
    pallas_call x1, Pallas kernels: 1.47 us -> 0.65 us  [finish(): pl.pallas_call(finish_kernel, name='finish', out_shape=(jax.ShapeDtypeStr...]
where the time goes in v3:
time: 45.2 us; the launch traced here: 45 us
  Pallas kernels  43.8 us (97%)
  between operations  1.29 us (3%)
    pallas_call x1, Pallas kernels, shards(): pl.pallas_call(functools.partial(kernel, group), name='step', out_shape=(...  43.1 us

profile of v3, /device:TPU:1, one launch (start us, length us, event | category | flops | bytes accessed | tf_op | source)
XLA Modules:
  0.0 45.0 jit_solution(11143372451062347991)
XLA Ops:
  1.3 43.1 %step.1 = (bf16[1,40,768]{2,1,0:T(8,128)(2,1)S(1)}, f32[8,40]{1,0:T(8,128)S(1)}) custom-call(s32[64]{0:T(128)} %lengths_hbm.1, s32[1,1]{1,0:T(1,128)} %bitcast.4.step_index_hbm, f32[1000]{0:T(1024)} %alphas_hbm.1, f32[1,128]{1,0:T(1,128)} %constant.2.clone.freq_hbm, f32[64]{0:T(128)} %q_gain_hbm.1, f32[64]{0:T(128)} %k_gain_hbm.1, ...), custom_call_target="tpu_custom_call" | custom-call | tf_op jit(solution)/shard_map/step/pallas_call | solution.py:555
  44.4 0.6 %finish.1 = (bf16[1,40,768]{2,1,0:T(8,128)(2,1)}, f32[8,40]{1,0:T(8,128)}) custom-call(bf16[1,40,768]{2,1,0:T(8,128)(2,1)S(1)} %get-tuple-element.6.hidden, f32[8,40]{1,0:T(8,128)S(1)} %get-tuple-element.7.latents), custom_call_target="tpu_custom_call" | custom-call | tf_op jit(solution)/shard_map/finish/pallas_call | solution.py:510

commit v4 on v3

--- a/solution.py
+++ b/solution.py
@@ -27,7 +27,7 @@
 head_eps = 1e-06
 final_eps = 1e-05
 LOW = -1e30
-QUERY, NEAR, OTHER_V, OTHER_K, FAR, STAT, OUT, PART, LAST = range(9)
+NEAR, PART, LAST, QUERY, OTHER, FAR, STAT, OUT = 0, 1, 2, 3, 6, 9, 12, 15
 MESH = pl.DeviceIdType.MESH
 F32 = jnp.float32
 BF16 = jnp.bfloat16
@@ -99,6 +99,8 @@
     obuf,
     ssend,
     sbuf,
+    sjoin,
+    acc,
     rsend,
     rbuf,
     fsend,
@@ -154,7 +156,8 @@
     ]
     load_k = load(keys_hbm.at[0], keys, 4)
     load_q = load(queries_hbm.at[0], queries, 5)
-    load_v = load(values_hbm.at[0], vbuf.at[own], 6)
+    for p in range(pairs):
+        load(values_hbm.at[0, :, pl.ds(p * PAIR, PAIR)], vbuf.at[p, own], 6)
     load_text = [load(text_keys_hbm.at[0], text_keys, 7), load(text_values_hbm.at[0], text_values, 8)]
     for j in range(group):
         load(weight_hbm.at[:, pl.ds(j * part, part)], weight.at[j], 9)
@@ -221,7 +224,7 @@
     load_k.wait()
     for p in range(pairs):
         made = rotate(head_norm(keys[:, pair_slice(p)], gain_k)).astype(BF16)
-        kbuf[own, :, pair_slice(p)] = made
+        kbuf[p, own] = made
     pl.semaphore_wait(barrier, len(everyone))
 
     def send(src, dst, kind, which, peer):
@@ -248,21 +251,23 @@
     def arrive(ref, which):
         whole_copy(ref, 0, which).wait_recv()
 
-    if NY > 1:
-        send(values_hbm.at[0], vbuf.at[own], 1, OTHER_V, y_peer)
-        send(kbuf.at[own], kbuf.at[own], 0, OTHER_K, y_peer)
-    for d in range(1, NX):
-        send(values_hbm.at[0], vbuf.at[own], 1, NEAR, x_peers[d - 1])
-        send(kbuf.at[own], kbuf.at[own], 0, NEAR, x_peers[d - 1])
+    for p in range(pairs):
+        if NY > 1:
+            for to in (y_peer,):
+                send(kbuf.at[p, own], kbuf.at[p, own], 0, OTHER + p, to)
+                send(values_hbm.at[0, :, pair_slice(p)], vbuf.at[p, own], 1, OTHER + p, to)
+    for p in range(pairs):
+        for to in x_peers:
+            send(kbuf.at[p, own], kbuf.at[p, own], 0, NEAR, to)
+            send(values_hbm.at[0, :, pair_slice(p)], vbuf.at[p, own], 1, NEAR, to)
 
     order_z = sorted(range(1, NZ), key=lambda d: -min(d, NZ - d))
     load_q.wait()
     for p in range(pairs):
         made = rotate(head_norm(queries[:, pair_slice(p)], gain_q)).astype(BF16)
-        qbuf[z, :, pair_slice(p)] = made
-
-    for d in order_z:
-        send(qbuf.at[z], qbuf.at[z], 2, QUERY, z_peers[d - 1])
+        qbuf[p, z] = made
+        for d in order_z:
+            send(qbuf.at[p, z], qbuf.at[p, z], 2, QUERY + p, z_peers[d - 1])
 
     for copy in load_text:
         copy.wait()
@@ -271,7 +276,7 @@
     text_stat = jnp.where(lax.rem(lane_row, 8) >= 6, 1.0, 0.0)
     for p in range(pairs):
         made = head_norm(text_keys[:, pair_slice(p)], gain_k)
-        query_part = qbuf[z, :, pair_slice(p)]
+        query_part = qbuf[p, z]
         value_part = text_values[:, pair_slice(p)]
         outs = []
         for which in range(2):
@@ -287,18 +292,20 @@
             text_stat = jnp.where(lane_row == 8 + head, count, text_stat)
         text_mixed.append(jnp.where(first_head, outs[0], outs[1]))
     below = jnp.zeros((LANES - ROWS, LANES), F32)
-    text_stat = jnp.concatenate([text_stat, below], axis=0).T[0:STATS]
-
-    if NY > 1:
-        arrive(vbuf.at[other], OTHER_V)
-        for d in range(1, NX):
-            send(vbuf.at[other], vbuf.at[other], 1, FAR, x_peers[d - 1])
-        arrive(kbuf.at[other], OTHER_K)
-        for d in range(1, NX):
-            send(kbuf.at[other], kbuf.at[other], 0, FAR, x_peers[d - 1])
-    arrive(qbuf.at[pl.ds(0, NZ - 1)], QUERY)
-    arrive(kbuf.at[pl.ds(0, 2 * (NX - 1))], NEAR)
-    load_v.wait()
+    text_stat = jnp.concatenate([text_stat, below], axis=0).T
+    lane_tile = lax.broadcasted_iota(jnp.int32, (8, LANES), 1)
+    text_stat = jnp.where(
+        lane_tile < HEAD, text_stat[0:8], pltpu.roll(text_stat[8:16], HEAD, 1)
+    )
+
+    for p in range(pairs):
+        if NY > 1:
+            arrive(kbuf.at[p, pl.ds(0, 2)], OTHER + p)
+            for to in x_peers:
+                send(kbuf.at[p, other], kbuf.at[p, other], 0, FAR + p, to)
+                send(vbuf.at[p, other], vbuf.at[p, other], 1, FAR + p, to)
+    arrive(kbuf.at[:, pl.ds(0, 2 * (NX - 1))], NEAR)
+    pltpu.make_async_copy(vbuf.at[:, 0], vbuf.at[:, 0], load_sem.at[6]).wait()
 
     n_keys = NX * ROWS
     n_queries = NZ * ROWS
@@ -306,7 +313,7 @@
     slot_row = lax.broadcasted_iota(jnp.int32, (ROWS, 1), 0)
 
     def gather(buf, p, yy):
-        blocks = [buf[j * NY + yy, :, pair_slice(p)].astype(F32) for j in range(NX)]
+        blocks = [buf[p, j * NY + yy].astype(F32) for j in range(NX)]
         return jnp.concatenate(blocks, axis=0)
 
     def live_of(yy):
@@ -331,40 +338,34 @@
     partials = []
     live = live_of(y)
     for p in range(pairs):
+        arrive(qbuf.at[p, pl.ds(0, NZ - 1)], QUERY + p)
         query_parts.append(
-            jnp.concatenate(
-                [qbuf[j, :, pair_slice(p)].astype(F32) for j in range(NZ)], axis=0
-            ).astype(BF16)
+            jnp.concatenate([qbuf[p, j].astype(F32) for j in range(NZ)], axis=0).astype(BF16)
         )
-    near = [score(p, y, live) for p in range(pairs)]
-    for p in range(pairs):
-        for scores, turned in near[p]:
+        for scores, turned in score(p, y, live):
             top = jnp.max(scores, axis=0, keepdims=True)
             weights = jnp.exp(scores - top)
             count = jnp.sum(weights, axis=0, keepdims=True)
             partials.append((top, count, nn(turned, weights.astype(BF16))))
 
-    if NY > 1:
-        arrive(kbuf.at[pl.ds(0, 2 * (NX - 1))], FAR)
     live = live_of(1 - y)
     stat_row = lax.broadcasted_iota(jnp.int32, (8, q_up), 0)
-    tops = jnp.zeros((8, q_up), F32)
-    counts = jnp.ones((8, q_up), F32)
-    lane_tile = lax.broadcasted_iota(jnp.int32, (8, LANES), 1)
 
     def widen(line):
         if q_up == n_queries:
             return line
         return jnp.concatenate([line, jnp.zeros((line.shape[0], q_up - n_queries), F32)], axis=1)
 
-    far = [score(p, 1 - y, live) for p in range(pairs)] if NY > 1 else None
     for p in range(pairs):
         outs = []
+        if NY > 1:
+            arrive(kbuf.at[p, pl.ds(0, 2 * (NX - 1))], FAR + p)
+            far = score(p, 1 - y, live)
         for which in range(2):
             head = 2 * p + which
             top, count, out = partials[head]
             if NY > 1:
-                scores, turned = far[p][which]
+                scores, turned = far[which]
                 before = top
                 top = jnp.maximum(before, jnp.max(scores, axis=0, keepdims=True))
                 fade = jnp.exp(before - top)
@@ -372,54 +373,54 @@
                 count = count * fade + jnp.sum(weights, axis=0, keepdims=True)
                 out = out * fade + nn(turned, weights.astype(BF16))
             outs.append(out)
-            tops = jnp.where(stat_row == head, widen(top), tops)
-            counts = jnp.where(stat_row == head, widen(count), counts)
+            tops = widen(top) if which == 0 else jnp.where(stat_row == 0, tops, widen(top))
+            counts = widen(count) if which == 0 else jnp.where(stat_row == 0, counts, widen(count))
         mixed = widen(jnp.concatenate(outs, axis=0)).T
         for j in range(NZ):
             osend[p, j] = mixed[j * ROWS : (j + 1) * ROWS].astype(BF16)
-        if p == pairs - 1:
-            for j in range(NZ):
-                left = pltpu.roll(tops, (q_up - j * ROWS) % q_up, 1)[:, 0:LANES]
-                right = pltpu.roll(counts, (q_up + HEAD - j * ROWS) % q_up, 1)[:, 0:LANES]
-                ssend[j] = jnp.where(lane_tile < HEAD, left, right)
-            for d in order_z:
-                zz = z_of[d - 1]
-                send(ssend.at[zz], sbuf.at[z], 3, STAT, z_peers[d - 1])
+        for j in range(NZ):
+            left = pltpu.roll(tops, (q_up - j * ROWS) % q_up, 1)[:, 0:LANES]
+            right = pltpu.roll(counts, (q_up + HEAD - j * ROWS) % q_up, 1)[:, 0:LANES]
+            ssend[p, j] = jnp.where(lane_tile < HEAD, left, right)[0:2]
         for d in order_z:
             zz = z_of[d - 1]
-            send(osend.at[p, zz], obuf.at[p, z], 4, OUT, z_peers[d - 1])
-
-    arrive(sbuf.at[pl.ds(0, NZ - 1)], STAT)
-    arrive(obuf.at[:, pl.ds(0, NZ - 1)], OUT)
-    tiles = [ssend[z]] + [sbuf[zz] for zz in z_of]
-    tops = tiles + [text_stat[0:8]]
-    counts = [pltpu.roll(tile, HEAD, 1) for tile in tiles] + [text_stat[8:16]]
-    top = functools.reduce(jnp.maximum, tops)
-    factors = [jnp.exp(one - top) for one in tops]
-    whole = sum(factor * count for factor, count in zip(factors, counts))
-    share = jnp.concatenate(
-        [factor / whole for factor in factors]
-        + [jnp.zeros((LANES - 8 * len(factors), LANES), F32)],
-        axis=0,
-    ).T
-    attended = []
-    for p in range(pairs):
+            send(ssend.at[p, zz], sbuf.at[p, z], 3, STAT + p, z_peers[d - 1])
+            send(osend.at[p, zz], obuf.at[p, z], 4, OUT + p, z_peers[d - 1])
+
+    pltpu.make_async_copy(weight, weight, load_sem.at[9]).wait()
+    for w in range(2):
+        sjoin[w] = jnp.where(lax.broadcasted_iota(jnp.int32, (16, LANES), 1) < HEAD, LOW, 0.0)
+    for p in range(pairs):
+        arrive(sbuf.at[p, pl.ds(0, NZ - 1)], STAT + p)
+        arrive(obuf.at[p, pl.ds(0, NZ - 1)], OUT + p)
+        stats = [ssend[p, z]] + [sbuf[p, zz] for zz in z_of] + [text_stat[2 * p : 2 * p + 2]]
+        for w in range(2):
+            for j, one in enumerate(stats):
+                sjoin[w, j : j + 1, :] = one[w : w + 1]
+        shares = []
+        for w in range(2):
+            found = sjoin[w]
+            count = pltpu.roll(found, HEAD, 1)
+            factor = jnp.exp(found - jnp.max(found, axis=0, keepdims=True))
+            shares.append(factor / jnp.sum(factor * count, axis=0, keepdims=True))
+        share = jnp.concatenate(shares + [jnp.zeros((LANES - 32, LANES), F32)], axis=0).T
         pieces = [osend[p, z]] + [obuf[p, zz] for zz in z_of]
         pieces = [piece.astype(F32) for piece in pieces] + [text_mixed[p]]
         joined = jnp.zeros((ROWS, PAIR), F32)
         for j, piece in enumerate(pieces):
-            lower = share[0:ROWS, 8 * j + 2 * p : 8 * j + 2 * p + 1]
-            upper = share[0:ROWS, 8 * j + 2 * p + 1 : 8 * j + 2 * p + 2]
+            lower = share[0:ROWS, j : j + 1]
+            upper = share[0:ROWS, 16 + j : 17 + j]
             joined = joined + piece * jnp.where(first_head, lower, upper)
-        attended.append(joined.astype(BF16))
-    attended = jnp.concatenate(attended, axis=1)
-
-    pltpu.make_async_copy(weight, weight, load_sem.at[9]).wait()
-    for d in sorted(range(1, group), reverse=True):
+        attended = joined.astype(BF16)
+        if p < pairs - 1:
+            for j in range(group):
+                more = nn(attended, weight[j, pair_slice(p), :])
+                acc[j] = more if p == 0 else acc[j] + more
+    for d in range(1, group):
         tt = t_of[d - 1]
-        rsend[d - 1] = nn(attended, weight[tt]).astype(BF16)
+        rsend[d - 1] = (acc[tt] + nn(attended, weight[tt, pair_slice(pairs - 1), :])).astype(BF16)
         send(rsend.at[d - 1], rbuf.at[t], 5, PART, t_peers[d - 1])
-    summed = nn(attended, weight[t])
+    summed = acc[t] + nn(attended, weight[t, pair_slice(pairs - 1), :])
     for copy in load_rest:
         copy.wait()
     lifted = 1.0 + scale[...].reshape(1, part)
@@ -481,10 +482,10 @@
     n_block = NX - 1 + (NX if NY > 1 else 0)
     for kind, ref in enumerate(
         [
-            kbuf.at[pl.ds(0, n_block)],
-            vbuf.at[pl.ds(0, n_block)],
-            qbuf.at[pl.ds(0, NZ - 1)],
-            sbuf.at[pl.ds(0, NZ - 1)],
+            kbuf.at[:, pl.ds(0, n_block)],
+            vbuf.at[:, pl.ds(0, n_block)],
+            qbuf.at[:, pl.ds(0, NZ - 1)],
+            sbuf.at[:, pl.ds(0, NZ - 1)],
             obuf.at[:, pl.ds(0, NZ - 1)],
             rbuf.at[pl.ds(0, group - 1)],
             fbuf.at[pl.ds(0, total - 1)],
@@ -579,20 +580,22 @@
             pltpu.VMEM((part,), F32),
             pltpu.VMEM((total * PIECE, part), F32),
             pltpu.VMEM((PIECE, ROWS), F32),
-            pltpu.VMEM((NZ, ROWS, width), BF16),
-            pltpu.VMEM((n_kv, ROWS, width), BF16),
-            pltpu.VMEM((n_kv, ROWS, width), BF16),
+            pltpu.VMEM((width // PAIR, NZ, ROWS, PAIR), BF16),
+            pltpu.VMEM((width // PAIR, n_kv, ROWS, PAIR), BF16),
+            pltpu.VMEM((width // PAIR, n_kv, ROWS, PAIR), BF16),
             pltpu.VMEM((width // PAIR, NZ, ROWS, PAIR), BF16),
             pltpu.VMEM((width // PAIR, NZ, ROWS, PAIR), BF16),
-            pltpu.VMEM((NZ, 8, LANES), F32),
-            pltpu.VMEM((NZ, 8, LANES), F32),
+            pltpu.VMEM((width // PAIR, NZ, 2, LANES), F32),
+            pltpu.VMEM((width // PAIR, NZ, 2, LANES), F32),
+            pltpu.VMEM((2, 16, LANES), F32),
+            pltpu.VMEM((group, ROWS, part), F32),
             pltpu.VMEM((max(group - 1, 1), ROWS, part), BF16),
             pltpu.VMEM((group, ROWS, part), BF16),
             pltpu.VMEM((total, 8, LANES), F32),
             pltpu.VMEM((total, 8, LANES), F32),
             dma((18,)),
             dma((7,)),
-            dma((9,)),
+            dma((18,)),
         ],
         compiler_params=pltpu.CompilerParams(collective_id=0, has_side_effects=True),
     )(

time: 45.2 us -> 43.9 us (0.971)
  Pallas kernels: 43.8 us -> 42.5 us
    pallas_call x1, Pallas kernels: 43.1 us -> 41.8 us  [shards(): pl.pallas_call(functools.partial(kernel, group), name='step', out_shape=(...]
where the time goes in v4:
time: 43.9 us; the launch traced here: 43.8 us
  Pallas kernels  42.5 us (97%)
  between operations  1.29 us (3%)
    pallas_call x1, Pallas kernels, shards(): pl.pallas_call(functools.partial(kernel, group), name='step', out_shape=(...  41.8 us

profile of v4, /device:TPU:1, one launch (start us, length us, event | category | flops | bytes accessed | tf_op | source)
XLA Modules:
  0.0 43.8 jit_solution(3703878431410194492)
XLA Ops:
  1.3 41.8 %step.1 = (bf16[1,40,768]{2,1,0:T(8,128)(2,1)S(1)}, f32[8,40]{1,0:T(8,128)S(1)}) custom-call(s32[64]{0:T(128)} %lengths_hbm.1, s32[1,1]{1,0:T(1,128)} %bitcast.4.step_index_hbm, f32[1000]{0:T(1024)} %alphas_hbm.1, f32[1,128]{1,0:T(1,128)} %constant.2.clone.freq_hbm, f32[64]{0:T(128)} %q_gain_hbm.1, f32[64]{0:T(128)} %k_gain_hbm.1, ...), custom_call_target="tpu_custom_call" | custom-call | tf_op jit(solution)/shard_map/step/pallas_call | solution.py:556
  43.1 0.6 %finish.1 = (bf16[1,40,768]{2,1,0:T(8,128)(2,1)}, f32[8,40]{1,0:T(8,128)}) custom-call(bf16[1,40,768]{2,1,0:T(8,128)(2,1)S(1)} %get-tuple-element.6.hidden, f32[8,40]{1,0:T(8,128)S(1)} %get-tuple-element.7.latents), custom_call_target="tpu_custom_call" | custom-call | tf_op jit(solution)/shard_map/finish/pallas_call | solution.py:511

commit v5 on v4

--- a/solution.py
+++ b/solution.py
@@ -225,6 +225,10 @@
     for p in range(pairs):
         made = rotate(head_norm(keys[:, pair_slice(p)], gain_k)).astype(BF16)
         kbuf[p, own] = made
+    load_q.wait()
+    for p in range(pairs):
+        made = rotate(head_norm(queries[:, pair_slice(p)], gain_q)).astype(BF16)
+        qbuf[p, z] = made
     pl.semaphore_wait(barrier, len(everyone))
 
     def send(src, dst, kind, which, peer):
@@ -262,10 +266,7 @@
             send(values_hbm.at[0, :, pair_slice(p)], vbuf.at[p, own], 1, NEAR, to)
 
     order_z = sorted(range(1, NZ), key=lambda d: -min(d, NZ - d))
-    load_q.wait()
-    for p in range(pairs):
-        made = rotate(head_norm(queries[:, pair_slice(p)], gain_q)).astype(BF16)
-        qbuf[p, z] = made
+    for p in range(pairs):
         for d in order_z:
             send(qbuf.at[p, z], qbuf.at[p, z], 2, QUERY + p, z_peers[d - 1])
 

time: 43.9 us -> 44 us (level)
  no operation moved by 1% of the time
where the time goes in v5:
time: 44 us; the launch traced here: 43.8 us
  Pallas kernels  42.5 us (97%)
  between operations  1.29 us (3%)
    pallas_call x1, Pallas kernels, shards(): pl.pallas_call(functools.partial(kernel, group), name='step', out_shape=(...  41.9 us

profile of v5, /device:TPU:1, one launch (start us, length us, event | category | flops | bytes accessed | tf_op | source)
XLA Modules:
  0.0 43.8 jit_solution(793495179487514075)
XLA Ops:
  1.3 41.9 %step.1 = (bf16[1,40,768]{2,1,0:T(8,128)(2,1)S(1)}, f32[8,40]{1,0:T(8,128)S(1)}) custom-call(s32[64]{0:T(128)} %lengths_hbm.1, s32[1,1]{1,0:T(1,128)} %bitcast.4.step_index_hbm, f32[1000]{0:T(1024)} %alphas_hbm.1, f32[1,128]{1,0:T(1,128)} %constant.2.clone.freq_hbm, f32[64]{0:T(128)} %q_gain_hbm.1, f32[64]{0:T(128)} %k_gain_hbm.1, ...), custom_call_target="tpu_custom_call" | custom-call | tf_op jit(solution)/shard_map/step/pallas_call | solution.py:557
  43.2 0.6 %finish.1 = (bf16[1,40,768]{2,1,0:T(8,128)(2,1)}, f32[8,40]{1,0:T(8,128)}) custom-call(bf16[1,40,768]{2,1,0:T(8,128)(2,1)S(1)} %get-tuple-element.6.hidden, f32[8,40]{1,0:T(8,128)S(1)} %get-tuple-element.7.latents), custom_call_target="tpu_custom_call" | custom-call | tf_op jit(solution)/shard_map/finish/pallas_call | solution.py:512

commit v6 on v5

--- a/solution.py
+++ b/solution.py
@@ -337,36 +337,35 @@
 
     query_parts = []
     partials = []
-    live = live_of(y)
-    for p in range(pairs):
+    live_near = live_of(y)
+    live_far = live_of(1 - y)
+    stat_row = lax.broadcasted_iota(jnp.int32, (8, q_up), 0)
+
+    def widen(line):
+        if q_up == n_queries:
+            return line
+        return jnp.concatenate([line, jnp.zeros((line.shape[0], q_up - n_queries), F32)], axis=1)
+
+    def near(p):
         arrive(qbuf.at[p, pl.ds(0, NZ - 1)], QUERY + p)
         query_parts.append(
             jnp.concatenate([qbuf[p, j].astype(F32) for j in range(NZ)], axis=0).astype(BF16)
         )
-        for scores, turned in score(p, y, live):
+        for scores, turned in score(p, y, live_near):
             top = jnp.max(scores, axis=0, keepdims=True)
             weights = jnp.exp(scores - top)
             count = jnp.sum(weights, axis=0, keepdims=True)
             partials.append((top, count, nn(turned, weights.astype(BF16))))
 
-    live = live_of(1 - y)
-    stat_row = lax.broadcasted_iota(jnp.int32, (8, q_up), 0)
-
-    def widen(line):
-        if q_up == n_queries:
-            return line
-        return jnp.concatenate([line, jnp.zeros((line.shape[0], q_up - n_queries), F32)], axis=1)
-
-    for p in range(pairs):
-        outs = []
+    def far(p):
+        outs, tops, counts = [], None, None
         if NY > 1:
             arrive(kbuf.at[p, pl.ds(0, 2 * (NX - 1))], FAR + p)
-            far = score(p, 1 - y, live)
+            scored = score(p, 1 - y, live_far)
         for which in range(2):
-            head = 2 * p + which
-            top, count, out = partials[head]
+            top, count, out = partials[2 * p + which]
             if NY > 1:
-                scores, turned = far[which]
+                scores, turned = scored[which]
                 before = top
                 top = jnp.maximum(before, jnp.max(scores, axis=0, keepdims=True))
                 fade = jnp.exp(before - top)
@@ -379,6 +378,9 @@
         mixed = widen(jnp.concatenate(outs, axis=0)).T
         for j in range(NZ):
             osend[p, j] = mixed[j * ROWS : (j + 1) * ROWS].astype(BF16)
+        for d in order_z:
+            zz = z_of[d - 1]
+            send(osend.at[p, zz], obuf.at[p, z], 4, OUT + p, z_peers[d - 1])
         for j in range(NZ):
             left = pltpu.roll(tops, (q_up - j * ROWS) % q_up, 1)[:, 0:LANES]
             right = pltpu.roll(counts, (q_up + HEAD - j * ROWS) % q_up, 1)[:, 0:LANES]
@@ -386,7 +388,12 @@
         for d in order_z:
             zz = z_of[d - 1]
             send(ssend.at[p, zz], sbuf.at[p, z], 3, STAT + p, z_peers[d - 1])
-            send(osend.at[p, zz], obuf.at[p, z], 4, OUT + p, z_peers[d - 1])
+
+    near(0)
+    for p in range(1, pairs):
+        near(p)
+        far(p - 1)
+    far(pairs - 1)
 
     pltpu.make_async_copy(weight, weight, load_sem.at[9]).wait()
     for w in range(2):

time: 44 us -> 44.5 us (1.011)
  Pallas kernels: 42.5 us -> 43.1 us
    pallas_call x1, Pallas kernels: 41.9 us -> 42.4 us  [shards(): pl.pallas_call(functools.partial(kernel, group), name='step', out_shape=(...]
where the time goes in v6:
time: 44.5 us; the launch traced here: 44.4 us
  Pallas kernels  43.1 us (97%)
  between operations  1.29 us (3%)
    pallas_call x1, Pallas kernels, shards(): pl.pallas_call(functools.partial(kernel, group), name='step', out_shape=(...  42.4 us

profile of v6, /device:TPU:1, one launch (start us, length us, event | category | flops | bytes accessed | tf_op | source)
XLA Modules:
  0.0 44.4 jit_solution(5295589042240048179)
XLA Ops:
  1.3 42.4 %step.1 = (bf16[1,40,768]{2,1,0:T(8,128)(2,1)S(1)}, f32[8,40]{1,0:T(8,128)S(1)}) custom-call(s32[64]{0:T(128)} %lengths_hbm.1, s32[1,1]{1,0:T(1,128)} %bitcast.4.step_index_hbm, f32[1000]{0:T(1024)} %alphas_hbm.1, f32[1,128]{1,0:T(1,128)} %constant.2.clone.freq_hbm, f32[64]{0:T(128)} %q_gain_hbm.1, f32[64]{0:T(128)} %k_gain_hbm.1, ...), custom_call_target="tpu_custom_call" | custom-call | tf_op jit(solution)/shard_map/step/pallas_call | solution.py:564
  43.7 0.6 %finish.1 = (bf16[1,40,768]{2,1,0:T(8,128)(2,1)}, f32[8,40]{1,0:T(8,128)}) custom-call(bf16[1,40,768]{2,1,0:T(8,128)(2,1)S(1)} %get-tuple-element.6.hidden, f32[8,40]{1,0:T(8,128)S(1)} %get-tuple-element.7.latents), custom_call_target="tpu_custom_call" | custom-call | tf_op jit(solution)/shard_map/finish/pallas_call | solution.py:519
